TPU v7x, 256 devices: a whole 4x4x8 slice. The times are simulated.
256 devices in a mesh: stream: 16 (over y_lo, z), azim: 4 (over x), slab: 4 (over y_hi, core).
Axes of the slice: x: 4, y: 4 (y_hi: 2, y_lo: 2; y = y_hi * 2 + y_lo), z: 8, core: 2. Of those that a mesh axis runs over, the one named last changes fastest.
Arguments:
- field: bfloat16 [8, 8, 4096, 256], P('azim', 'slab', 'stream'), may hold values from -6 to 6
- gain_stream: float32 [256], replicated, may hold values from 0.5 to 1.5
- gain_cross: float32 [256], replicated, may hold values from 0.5 to 1.5
- stream_query: bfloat16 [256, 256], replicated, may hold values from -0.375 to 0.375
- stream_key: bfloat16 [256, 256], replicated, may hold values from -0.375 to 0.375
- stream_value: bfloat16 [256, 256], replicated, may hold values from -0.375 to 0.375
- stream_out: bfloat16 [256, 256], replicated, may hold values from -0.375 to 0.375
- cross_query: bfloat16 [256, 256], replicated, may hold values from -0.375 to 0.375
- cross_key: bfloat16 [256, 256], replicated, may hold values from -0.375 to 0.375
- cross_value: bfloat16 [256, 256], replicated, may hold values from -0.375 to 0.375
- cross_out: bfloat16 [256, 256], replicated, may hold values from -0.375 to 0.375
- stream_scale: float32 [4], replicated, may hold values from 10 to 30
- cross_scale: float32 [4], replicated, may hold values from 10 to 30
- azim_bias: float32 [4, 8], replicated, may hold values from -3 to 3
- azim_order: int32 [8], replicated, may hold values from 0 to 7, each once
- block_lists: int32 [32, 4], P('stream'), may hold values from 0 to 31, as said below
Outputs:
- layer_out: bfloat16 [8, 8, 4096, 256], P('azim', 'slab', 'stream')
Inputs may be any that keep to these rules, and one draw needn't show every extreme that they name: `block_lists`: blocks are numbered along the line, 2 to a device in order. Each entry of row b is block c of the device e steps away, along the closed streamwise loop, from the device of block b, with |e| <= 2 and 0 <= c < 2; the blocks named in a row are distinct. `azim_order`: A permutation of the 8 azimuthal positions.
All inputs are finite; a program needn't handle non-finite values.
Results may differ from a plain program's by a relative error of at most 0.011.
Values may be sent and summed in bfloat16 or wider, within the bound.
No kernel may reach another device: no remote copies, remote signals or barrier semaphores. Data moves between devices by JAX's collectives and lax.ppermute only.
A program may use at most 64 MiB of HBM per device.

v0:
```python
import jax
import jax.numpy as jnp
from jax import lax
from jax.sharding import PartitionSpec as P

D = 256
HEADS = 4
HEAD_DIM = 64
BLOCK = 128
REACH = 2
LIST_LEN = 4
BLOCKS_DEV = 2


def shifted(block, axis, distance):
    devices = range(lax.axis_size(axis))
    route = [((i - distance) % len(devices), i) for i in devices]
    return lax.ppermute(block, axis, route)


def norm_rows(values, gain_row):
    floats = values.astype(jnp.float32)
    scaled = floats * lax.rsqrt(jnp.mean(floats * floats, axis=-1, keepdims=True) + 1e-05)
    return (scaled * gain_row).astype(jnp.bfloat16)


def project(row_block, weight):
    flattened = row_block.reshape(-1, row_block.shape[-1])
    product = jnp.dot(flattened, weight, preferred_element_type=jnp.float32)
    return product.reshape(row_block.shape[:-1] + (weight.shape[1],))


def head_unit(values, scales):
    shaped = values.reshape(values.shape[:-1] + (HEADS, HEAD_DIM))
    shaped = shaped * lax.rsqrt(jnp.mean(shaped * shaped, axis=-1, keepdims=True) + 1e-06)
    if scales is not None:
        shaped = shaped * (scales / HEAD_DIM)[:, None]
    return shaped.reshape(values.shape).astype(jnp.bfloat16)


def section_bias(azim_bias, azim_order, radials):
    azimuths = azim_order.shape[0]
    distance = (azim_order[:, None] - azim_order[None, :]) % azimuths
    onehot = (distance[:, :, None] == jnp.arange(azimuths, dtype=jnp.int32)[None, None, :]).astype(
        jnp.float32
    )
    lookup = jnp.einsum("abm,hm->hab", onehot, azim_bias, precision=lax.Precision.HIGHEST)
    lookup = jnp.broadcast_to(
        lookup[:, :, None, :, None], (HEADS, azimuths, radials, azimuths, radials)
    )
    return lookup.reshape(HEADS, azimuths * radials, azimuths * radials)


def per_device(
    field,
    gain_stream,
    gain_cross,
    stream_query,
    stream_key,
    stream_value,
    stream_out,
    cross_query,
    cross_key,
    cross_value,
    cross_out,
    stream_scale,
    cross_scale,
    azim_bias,
    azim_order,
    block_lists,
):
    line_count = field.shape[0] * field.shape[1]
    length = field.shape[2]
    tokens = field.reshape(line_count, length, D)
    normed = norm_rows(tokens, gain_stream)
    queries = head_unit(project(normed, stream_query), stream_scale)
    query_heads = queries.reshape(line_count, BLOCKS_DEV, BLOCK, HEADS, HEAD_DIM)
    key_part = head_unit(project(normed, stream_key), None)
    value_part = project(normed, stream_value).astype(jnp.bfloat16)
    payload = jnp.concatenate([key_part, value_part], axis=-1)
    cycle_size = lax.axis_size("stream")
    position = lax.axis_index("stream")
    visited = [0]
    forward = []
    backward = []
    for stride in range(1, REACH + 1):
        visited.append(stride % cycle_size)
        forward.append(stride)
    for stride in range(1, REACH + 1):
        visited.append(-stride % cycle_size)
        backward.append(stride)
    pieces = [payload]
    sources = [position]
    for offset in forward + [-stride for stride in backward]:
        arrived = shifted(payload, "stream", offset)
        pieces.append(arrived)
        sources.append((position - offset) % cycle_size)
    source_count = len(pieces)
    window_buffer = jnp.concatenate(
        [piece.reshape(line_count, BLOCKS_DEV, BLOCK, 2 * D) for piece in pieces], axis=1
    )
    source_ids = jnp.stack([jnp.asarray(source, jnp.int32) for source in sources])
    listed_device = block_lists // BLOCKS_DEV
    slot_match = (listed_device[:, :, None] == source_ids[None, None, :]).astype(jnp.int32)
    slot = jnp.sum(slot_match * jnp.arange(source_count, dtype=jnp.int32)[None, None, :], axis=-1)
    buffer_index = (slot * BLOCKS_DEV + block_lists % BLOCKS_DEV).reshape(-1)
    picked = jnp.take(window_buffer, buffer_index, axis=1).reshape(
        line_count, BLOCKS_DEV, LIST_LEN * BLOCK, 2 * D
    )
    key_heads = picked[..., :D].reshape(line_count, BLOCKS_DEV, LIST_LEN * BLOCK, HEADS, HEAD_DIM)
    value_heads = picked[..., D:].reshape(line_count, BLOCKS_DEV, LIST_LEN * BLOCK, HEADS, HEAD_DIM)
    scores = jnp.einsum(
        "lbqhd,lbkhd->lbhqk", query_heads, key_heads, preferred_element_type=jnp.float32
    )
    weights = jnp.exp(scores)
    totals = jnp.sum(weights, axis=-1)
    weighted = jnp.einsum(
        "lbhqk,lbkhd->lbqhd",
        weights.astype(jnp.bfloat16),
        value_heads,
        preferred_element_type=jnp.float32,
    )
    attended = (
        (weighted / jnp.transpose(totals, (0, 1, 3, 2))[..., None])
        .reshape(line_count, length, D)
        .astype(jnp.bfloat16)
    )
    after_stream = (tokens.astype(jnp.float32) + project(attended, stream_out)).astype(jnp.bfloat16)
    layout = norm_rows(after_stream, gain_cross).reshape(field.shape)
    section = lax.all_to_all(
        lax.all_to_all(layout, "azim", split_axis=2, concat_axis=0, tiled=True),
        "slab",
        split_axis=2,
        concat_axis=1,
        tiled=True,
    )
    azimuths = section.shape[0]
    radials = section.shape[1]
    row_count = section.shape[2]
    section_tokens = azimuths * radials
    cross_queries = head_unit(project(section, cross_query), cross_scale).reshape(
        section_tokens, row_count, HEADS, HEAD_DIM
    )
    cross_keys = head_unit(project(section, cross_key), None).reshape(
        section_tokens, row_count, HEADS, HEAD_DIM
    )
    cross_values = (
        project(section, cross_value)
        .astype(jnp.bfloat16)
        .reshape(section_tokens, row_count, HEADS, HEAD_DIM)
    )
    biases = section_bias(azim_bias, azim_order, radials)
    cross_scores = (
        jnp.einsum("aqhd,bqhd->qhab", cross_queries, cross_keys, preferred_element_type=jnp.float32)
        + biases[None]
    )
    cross_weights = jnp.exp(cross_scores)
    cross_totals = jnp.sum(cross_weights, axis=-1)
    cross_weighted = jnp.einsum(
        "qhab,bqhd->aqhd",
        cross_weights.astype(jnp.bfloat16),
        cross_values,
        preferred_element_type=jnp.float32,
    )
    crossed = (cross_weighted / jnp.transpose(cross_totals, (2, 0, 1))[..., None]).astype(
        jnp.bfloat16
    )
    crossed = crossed.reshape(azimuths, radials, row_count, D)
    returned = lax.all_to_all(
        lax.all_to_all(crossed, "slab", split_axis=1, concat_axis=2, tiled=True),
        "azim",
        split_axis=0,
        concat_axis=2,
        tiled=True,
    )
    returned = returned.reshape(line_count, length, D)
    result = (after_stream.astype(jnp.float32) + project(returned, cross_out)).astype(jnp.bfloat16)
    return result.reshape(field.shape)


def solution(mesh):
    in_specs = (
        P("azim", "slab", "stream", None),
        P(),
        P(),
        P(),
        P(),
        P(),
        P(),
        P(),
        P(),
        P(),
        P(),
        P(),
        P(),
        P(),
        P(),
        P("stream", None),
    )
    out_specs = P("azim", "slab", "stream", None)
    return jax.shard_map(
        per_device, mesh=mesh, in_specs=in_specs, out_specs=out_specs, check_vma=False
    )
```

profile of v0, /device:TPU:32, one launch (start us, length us, event | category | flops | bytes accessed | tf_op | source)
XLA Modules:
  0.0 185.3 jit_solution(8032317681956199737)
XLA Ops:
  4.3 2.0 %collective-permute-start = (bf16[4,256,512]{1,2,0:T(8,128)(2,1)S(1)}, bf16[4,256,512]{1,2,0:T(8,128)(2,1)}, u32[]{:S(2)}, u32[]{:S(2)}) collective-permute-start(bf16[4,256,512]{1,2,0:T(8,128)(2,1)S(1)} %pad_maximum_fusion), channel_id=1, source_target_pairs={{240,0},{0,16},{16,32},{32,48},{48,64},{64,80},{80,96},{96,112},{1... | collective-permute-start | bytes 3145736 | tf_op jit(solution)/shard_map/ppermute | solution.py:18
  6.3 4.5 %collective-permute-start.1 = (bf16[4,256,512]{1,2,0:T(8,128)(2,1)S(1)}, bf16[4,256,512]{1,2,0:T(8,128)(2,1)}, u32[]{:S(2)}, u32[]{:S(2)}) collective-permute-start(bf16[4,256,512]{1,2,0:T(8,128)(2,1)S(1)} %pad_maximum_fusion), channel_id=1, source_target_pairs={{224,0},{240,16},{0,32},{16,48},{32,64},{48,80},{64,96},{80,112},{... | collective-permute-start | bytes 3145736 | tf_op jit(solution)/shard_map/ppermute | solution.py:18
  10.8 2.0 %collective-permute-start.3 = (bf16[4,256,512]{1,2,0:T(8,128)(2,1)S(1)}, bf16[4,256,512]{1,2,0:T(8,128)(2,1)}, u32[]{:S(2)}, u32[]{:S(2)}) collective-permute-start(bf16[4,256,512]{1,2,0:T(8,128)(2,1)S(1)} %pad_maximum_fusion), channel_id=1, source_target_pairs={{32,0},{48,16},{64,32},{80,48},{96,64},{112,80},{128,96},{144,112}... | collective-permute-start | bytes 3145736 | tf_op jit(solution)/shard_map/ppermute | solution.py:18
  14.8 2.3 %constant_dynamic-update-slice_fusion.4 = bf16[4,10,128,512]{3,2,1,0:T(8,128)(2,1)} fusion(bf16[4,2,128,512]{3,2,1,0:T(8,128)(2,1)} %bitcast.161), kind=kLoop, calls=%fused_computation.62 | loop fusion | bytes 2097152
  18.5 15.6 %collective-permute-done = bf16[4,256,512]{1,2,0:T(8,128)(2,1)} collective-permute-done((bf16[4,256,512]{1,2,0:T(8,128)(2,1)S(1)}, bf16[4,256,512]{1,2,0:T(8,128)(2,1)}, u32[]{:S(2)}, u32[]{:S(2)}) %collective-permute-start) | collective-permute-done | bytes 1048608 | tf_op jit(solution)/shard_map/ppermute | solution.py:18
  35.5 43.5 %collective-permute-done.1 = bf16[4,256,512]{1,2,0:T(8,128)(2,1)} collective-permute-done((bf16[4,256,512]{1,2,0:T(8,128)(2,1)S(1)}, bf16[4,256,512]{1,2,0:T(8,128)(2,1)}, u32[]{:S(2)}, u32[]{:S(2)}) %collective-permute-start.1) | collective-permute-done | bytes 1048608 | tf_op jit(solution)/shard_map/ppermute | solution.py:18
  79.0 2.3 %copy.183 = bf16[4,256,512]{2,1,0:T(8,128)(2,1)} copy(bf16[4,256,512]{1,2,0:T(8,128)(2,1)} %collective-permute-done.1) | data formatting | bytes 2097152 | tf_op jit(solution)/shard_map/reshape | solution.py:100
  81.3 2.3 %copy.184 = bf16[4,256,512]{2,1,0:T(8,128)(2,1)} copy(bf16[4,256,512]{1,2,0:T(8,128)(2,1)} %collective-permute-done.2) | data formatting | bytes 2097152 | tf_op jit(solution)/shard_map/reshape | solution.py:100
  90.2 5.3 %gather_fusion = bf16[8,4,128,512]{3,2,1,0:T(8,128)(2,1)} fusion(bf16[4,10,128,512]{3,2,1,0:T(8,128)(2,1)} %constant_dynamic-update-slice_fusion, s32[1024]{0:T(1024)S(1)} %pad_clamp_fusion), kind=kCustom, calls=%fused_computation | custom fusion | bytes 8388640 | tf_op jit(solution)/shard_map/jit(_take)/gather | solution.py:107
  95.5 2.5 %copy.141 = bf16[4,8,128,512]{3,2,1,0:T(8,128)(2,1)S(1)} copy(bf16[4,8,128,512]{3,2,0,1:T(8,128)(2,1)} %bitcast.148) | data formatting | bytes 8388608 | tf_op jit(solution)/shard_map/jit(_take)/gather | solution.py:107
  98.4 1.8 fusion.34
  100.2 2.4 %copy.144 = bf16[4,2,512,256]{2,3,1,0:T(8,128)(2,1)} copy(bf16[4,2,512,256]{3,2,1,0:T(8,128)(2,1)S(1)} %get-tuple-element.7) | data formatting | bytes 4194304 | tf_op jit(solution)/shard_map/slice | solution.py:110
  102.5 2.8 %copy.142 = bf16[4,2,512,256]{2,3,1,0:T(8,128)(2,1)S(1)} copy(bf16[4,2,512,256]{3,2,1,0:T(8,128)(2,1)} %get-tuple-element.8) | data formatting | bytes 4194304 | tf_op jit(solution)/shard_map/slice | solution.py:111
  105.3 3.6 %exponential_reduce_fusion = (f32[4,2,4,128]{3,2,1,0:T(4,128)S(1)}, f32[4,2,4,128,512]{4,3,2,1,0:T(8,128)S(1)}) fusion(bf16[4,2,512,4,64]{2,4,3,1,0:T(8,128)(2,1)} %bitcast.151, f32[4,256,4,64]{1,3,2,0:T(8,128)} %get-tuple-element.12, f32[4]{0:T(128)S(1)} %broadcast_multiply_fusion.1, f32[4,256,4]{1,2,0:T(4,128)S(1)} %add_rsqrt_fusion.2), kind=kOutput, calls=%fused_computation.1 | convolution fusion | flops 271314944 | bytes 11567120 | tf_op jit(solution)/shard_map/lbqhd,lbkhd->lbhqk/dot_general | solution.py:112
  114.0 4.3 %all-to-all-start = ((bf16[2,2,256,256]{3,1,0,2:T(2,128)(2,1)}), bf16[2,2,256,256]{3,1,0,2:T(2,128)(2,1)S(1)}, u32[]{:S(2)}, u32[]{:S(2)}) async-start(bf16[2,2,256,256]{3,1,0,2:T(2,128)(2,1)} %copy.149), calls=%async_computation | async-start | bytes 1048576 | tf_op jit(solution)/shard_map/all_to_all | solution.py:131
  119.2 7.9 %all-to-all-done = bf16[2,2,256,256]{3,1,0,2:T(2,128)(2,1)S(1)} async-done(((bf16[2,2,256,256]{3,1,0,2:T(2,128)(2,1)}), bf16[2,2,256,256]{3,1,0,2:T(2,128)(2,1)S(1)}, u32[]{:S(2)}, u32[]{:S(2)}) %all-to-all-start) | async-done | bytes 524320 | tf_op jit(solution)/shard_map/all_to_all | solution.py:131
  128.6 4.2 %all-to-all-start.1 = ((bf16[8,2,64,256]{3,1,0,2:T(2,128)(2,1)}), bf16[8,2,64,256]{3,1,0,2:T(2,128)(2,1)S(1)}, u32[]{:S(2)}, u32[]{:S(2)}) async-start(bf16[8,2,64,256]{3,1,0,2:T(2,128)(2,1)} %copy.152), calls=%async_computation.1 | async-start | bytes 1048576 | tf_op jit(solution)/shard_map/all_to_all | solution.py:130
  133.8 9.4 %all-to-all-done.1 = bf16[8,2,64,256]{3,1,0,2:T(2,128)(2,1)S(1)} async-done(((bf16[8,2,64,256]{3,1,0,2:T(2,128)(2,1)}), bf16[8,2,64,256]{3,1,0,2:T(2,128)(2,1)S(1)}, u32[]{:S(2)}, u32[]{:S(2)}) %all-to-all-start.1) | async-done | bytes 524320 | tf_op jit(solution)/shard_map/all_to_all | solution.py:130
  143.3 1.8 multiply_reduce_fusion.1
  145.8 2.0 %multiply_reduce_fusion = (f32[8,8,16,4]{2,3,1,0:T(4,128)S(1)}, f32[8,8,16,4,64]{4,2,3,1,0:T(8,128)}) fusion(bf16[8,8,16,256,1]{3,2,4,1,0:T(8,128)(2,1)S(1)} %bitcast.153, bf16[4,64,256,1,1]{2,1,0,4,3:T(8,128)(2,1)S(1)} %bitcast.174), kind=kOutput, calls=%fused_computation.9 | convolution fusion | flops 134737920 | bytes 1720320 | tf_op jit(solution)/shard_map/dot_general | solution.py:29
  150.2 1.9 %multiply_convert_fusion = bf16[8,8,16,4,64]{4,2,3,1,0:T(8,128)(2,1)S(1)} fusion(f32[8,8,16,4,64]{4,2,3,1,0:T(8,128)} %get-tuple-element.18, f32[8,8,16,4]{2,3,1,0:T(4,128)} %add_rsqrt_fusion), kind=kLoop, calls=%fused_computation.8 | loop fusion | flops 524288 | bytes 1589248 | tf_op jit(solution)/shard_map/convert_element_type | solution.py:38
  153.0 2.6 %fusion.2 = (f32[16,4,64]{2,1,0:T(4,128)S(1)}, f32[16,4,64,64]{2,3,1,0:T(8,128)S(1)}) fusion(f32[4,64,64]{1,2,0:T(8,128)S(1)} %add.135, bf16[64,16,4,64]{3,1,2,0:T(8,128)(2,1)S(1)} %bitcast.159, bf16[64,16,4,64]{3,1,2,0:T(8,128)(2,1)S(1)} %bitcast.163), kind=kOutput, calls=%fused_computation.12 | convolution fusion | flops 34074624 | bytes 2179072 | tf_op jit(solution)/shard_map/aqhd,bqhd->qhab/dot_general | solution.py:154
  159.2 12.8 %all_to_all.66 = bf16[8,8,16,256]{3,2,0,1:T(8,128)(2,1)S(1)} all-to-all(bf16[8,8,16,256]{3,2,0,1:T(8,128)(2,1)S(1)} %copy.163), channel_id=1, replica_groups=mesh['stream'=16,'azim'=4,'slab'=4] {'slab'}, dimensions={1} | all-to-all | bytes 1048576 | tf_op jit(solution)/shard_map/all_to_all | solution.py:170
  172.1 11.8 %all_to_all.67 = bf16[8,2,64,256]{3,2,1,0:T(8,128)(2,1)S(1)} all-to-all(bf16[8,2,64,256]{3,2,1,0:T(8,128)(2,1)S(1)} %bitcast.172), channel_id=1, replica_groups=mesh['stream'=16,'azim'=4,'slab'=4] {'azim'}, dimensions={0} | all-to-all | bytes 1048576 | tf_op jit(solution)/shard_map/all_to_all | solution.py:169
  (113 shorter events, 33.1 us)
Async XLA Ops:
  0.0 111.4 %copy-start = (bf16[256,256]{1,0:T(8,128)(2,1)S(1)}, bf16[256,256]{1,0:T(8,128)(2,1)}, u32[]{:S(2)}) copy-start(bf16[256,256]{1,0:T(8,128)(2,1)} %param.22) | copy-start | bytes 393220
  0.0 2.6 %copy-start.1 = (bf16[2,2,256,256]{3,2,1,0:T(8,128)(2,1)S(1)}, bf16[2,2,256,256]{3,2,1,0:T(8,128)(2,1)}, u32[]{:S(2)}) copy-start(bf16[2,2,256,256]{3,2,1,0:T(8,128)(2,1)} %param.16) | copy-start | bytes 1572868
  0.0 2.6 %copy-start.16 = (f32[256]{0:T(256)S(1)}, f32[256]{0:T(256)}, u32[]{:S(2)}) copy-start(f32[256]{0:T(256)} %param.17) | copy-start | bytes 3076
  0.0 2.9 %copy-start.10 = (bf16[256,256]{1,0:T(8,128)(2,1)S(1)}, bf16[256,256]{1,0:T(8,128)(2,1)}, u32[]{:S(2)}) copy-start(bf16[256,256]{1,0:T(8,128)(2,1)} %param.20) | copy-start | bytes 393220
  3.5 9.4 %copy-start.15 = (s32[2,4]{1,0:T(2,128)S(1)}, s32[2,4]{1,0:T(2,128)}, u32[]{:S(2)}) copy-start(s32[2,4]{1,0:T(2,128)} %param.31) | copy-start | bytes 100
  3.9 9.4 %copy-start.20 = (f32[4]{0:T(128)S(1)}, f32[4]{0:T(128)}, u32[]{:S(2)}) copy-start(f32[4]{0:T(128)} %param.27) | copy-start | bytes 52
  4.2 10.5 %copy-start.11 = (bf16[256,256]{1,0:T(8,128)(2,1)S(1)}, bf16[256,256]{1,0:T(8,128)(2,1)}, u32[]{:S(2)}) copy-start(bf16[256,256]{1,0:T(8,128)(2,1)} %param.19) | copy-start | bytes 393220
  4.3 29.7 %collective-permute-start = (bf16[4,256,512]{1,2,0:T(8,128)(2,1)S(1)}, bf16[4,256,512]{1,2,0:T(8,128)(2,1)}, u32[]{:S(2)}, u32[]{:S(2)}) collective-permute-start(bf16[4,256,512]{1,2,0:T(8,128)(2,1)S(1)} %pad_maximum_fusion), channel_id=1, source_target_pairs={{240,0},{0,16},{16,32},{32,48},{48,64},{64,80},{80,96},{96,112},{1... | collective-permute-start | bytes 3145736 | tf_op jit(solution)/shard_map/ppermute | solution.py:18
  6.3 72.7 %collective-permute-start.1 = (bf16[4,256,512]{1,2,0:T(8,128)(2,1)S(1)}, bf16[4,256,512]{1,2,0:T(8,128)(2,1)}, u32[]{:S(2)}, u32[]{:S(2)}) collective-permute-start(bf16[4,256,512]{1,2,0:T(8,128)(2,1)S(1)} %pad_maximum_fusion), channel_id=1, source_target_pairs={{224,0},{240,16},{0,32},{16,48},{32,64},{48,80},{64,96},{80,112},{... | collective-permute-start | bytes 3145736 | tf_op jit(solution)/shard_map/ppermute | solution.py:18
  10.8 70.5 %collective-permute-start.2 = (bf16[4,256,512]{1,2,0:T(8,128)(2,1)S(1)}, bf16[4,256,512]{1,2,0:T(8,128)(2,1)}, u32[]{:S(2)}, u32[]{:S(2)}) collective-permute-start(bf16[4,256,512]{1,2,0:T(8,128)(2,1)S(1)} %pad_maximum_fusion), channel_id=1, source_target_pairs={{16,0},{32,16},{48,32},{64,48},{80,64},{96,80},{112,96},{128,112},... | collective-permute-start | bytes 3145736 | tf_op jit(solution)/shard_map/ppermute | solution.py:18
  10.8 76.7 %collective-permute-start.3 = (bf16[4,256,512]{1,2,0:T(8,128)(2,1)S(1)}, bf16[4,256,512]{1,2,0:T(8,128)(2,1)}, u32[]{:S(2)}, u32[]{:S(2)}) collective-permute-start(bf16[4,256,512]{1,2,0:T(8,128)(2,1)S(1)} %pad_maximum_fusion), channel_id=1, source_target_pairs={{32,0},{48,16},{64,32},{80,48},{96,64},{112,80},{128,96},{144,112}... | collective-permute-start | bytes 3145736 | tf_op jit(solution)/shard_map/ppermute | solution.py:18
  83.7 2.7 %copy-start.5 = (bf16[4,256,512]{2,1,0:T(8,128)(2,1)S(1)}, bf16[4,256,512]{2,1,0:T(8,128)(2,1)}, u32[]{:S(2)}) copy-start(bf16[4,256,512]{2,1,0:T(8,128)(2,1)} %copy.184) | copy-start | bytes 3145732
  111.8 6.4 %copy-start.12 = (bf16[256,256]{1,0:T(8,128)(2,1)S(1)}, bf16[256,256]{1,0:T(8,128)(2,1)}, u32[]{:S(2)}) copy-start(bf16[256,256]{1,0:T(8,128)(2,1)} %param.23) | copy-start | bytes 393220
  111.8 7.2 %copy-start.13 = (bf16[256,256]{1,0:T(8,128)(2,1)S(1)}, bf16[256,256]{1,0:T(8,128)(2,1)}, u32[]{:S(2)}) copy-start(bf16[256,256]{1,0:T(8,128)(2,1)} %param.24) | copy-start | bytes 393220
  111.8 7.3 %copy-start.17 = (s32[8]{0:T(128)S(1)}, s32[8]{0:T(128)}, u32[]{:S(2)}) copy-start(s32[8]{0:T(128)} %param.30) | copy-start | bytes 100
  114.0 13.2 %all-to-all-start = ((bf16[2,2,256,256]{3,1,0,2:T(2,128)(2,1)}), bf16[2,2,256,256]{3,1,0,2:T(2,128)(2,1)S(1)}, u32[]{:S(2)}, u32[]{:S(2)}) async-start(bf16[2,2,256,256]{3,1,0,2:T(2,128)(2,1)} %copy.149), calls=%async_computation | async-start | bytes 1048576 | tf_op jit(solution)/shard_map/all_to_all | solution.py:131
  119.2 13.6 %copy-start.19 = (f32[4,8]{1,0:T(4,128)S(1)}, f32[4,8]{1,0:T(4,128)}, u32[]{:S(2)}) copy-start(f32[4,8]{1,0:T(4,128)} %param.29) | copy-start | bytes 388
  127.3 6.5 %copy-start.21 = (f32[4]{0:T(128)S(1)}, f32[4]{0:T(128)}, u32[]{:S(2)}) copy-start(f32[4]{0:T(128)} %param.28) | copy-start | bytes 52
  128.6 14.5 %all-to-all-start.1 = ((bf16[8,2,64,256]{3,1,0,2:T(2,128)(2,1)}), bf16[8,2,64,256]{3,1,0,2:T(2,128)(2,1)S(1)}, u32[]{:S(2)}, u32[]{:S(2)}) async-start(bf16[8,2,64,256]{3,1,0,2:T(2,128)(2,1)} %copy.152), calls=%async_computation.1 | async-start | bytes 1048576 | tf_op jit(solution)/shard_map/all_to_all | solution.py:130
  145.1 3.5 %copy-start.9 = (bf16[256,256]{1,0:T(8,128)(2,1)S(1)}, bf16[256,256]{1,0:T(8,128)(2,1)}, u32[]{:S(2)}) copy-start(bf16[256,256]{1,0:T(8,128)(2,1)} %param.25) | copy-start | bytes 393220
  148.8 3.4 %copy-start.7 = (f32[8,8,16,4]{2,3,1,0:T(4,128)S(1)}, f32[8,8,16,4]{2,3,1,0:T(4,128)}, u32[]{:S(2)}) copy-start(f32[8,8,16,4]{2,3,1,0:T(4,128)} %add_rsqrt_fusion.1) | copy-start | bytes 49156
  152.9 2.6 %copy-start.6 = (bf16[64,16,4,64]{3,2,1,0:T(4,128)(2,1)S(1)}, bf16[64,16,4,64]{3,2,1,0:T(4,128)(2,1)}, u32[]{:S(2)}) copy-start(bf16[64,16,4,64]{3,2,1,0:T(4,128)(2,1)} %reshape.288) | copy-start | bytes 1572868
  159.2 24.8 %copy-start.3 = (bf16[4,256,256]{1,2,0:T(8,128)(2,1)S(1)}, bf16[4,256,256]{1,2,0:T(8,128)(2,1)}, u32[]{:S(2)}) copy-start(bf16[4,256,256]{1,2,0:T(8,128)(2,1)} %copy-done.2) | copy-start | bytes 1572868
  159.2 24.8 %copy-start.14 = (bf16[256,256]{1,0:T(8,128)(2,1)S(1)}, bf16[256,256]{1,0:T(8,128)(2,1)}, u32[]{:S(2)}) copy-start(bf16[256,256]{1,0:T(8,128)(2,1)} %param.26) | copy-start | bytes 393220
  (4 other events, 5.4 us)
where the time goes:
time: 186 us; the launch traced here: 185 us
  waiting for transfers between devices  76.4 us (41%)
  local copies, waits for them, and re-layouts  43.7 us (23%)
  blocking collectives  24.6 us (13%)
  starting transfers between devices  17 us (9%)
  matrix products  16.2 us (9%)
  other arithmetic  6.9 us (4%)
    ppermute x4, waiting for transfers between devices, shifted(): return lax.ppermute(block, axis, route)  59.1 us
    all_to_all x1, blocking collectives, per_device(): lax.all_to_all(crossed, 'slab', split_axis=1, concat_axis=2, tiled=True)  12.8 us
    all_to_all x1, blocking collectives, per_device(): lax.all_to_all(lax.all_to_all(crossed, 'slab', split_axis=1, concat_axis=...  11.8 us
    all_to_all x1, waiting for transfers between devices, per_device(): lax.all_to_all(lax.all_to_all(layout, 'azim', split_axis=2, concat_axis=0...  9.35 us
    reshape x5, local copies, waits for them, and re-layouts, per_device(): piece.reshape(line_count, BLOCKS_DEV, BLOCK, 2 * D)  8.95 us
    ppermute x4, starting transfers between devices, shifted(): return lax.ppermute(block, axis, route)  8.52 us
    unnamed x54, local copies, waits for them, and re-layouts  8.4 us
    all_to_all x1, waiting for transfers between devices, per_device(): lax.all_to_all(layout, 'azim', split_axis=2, concat_axis=0, tiled=True)  7.94 us
  transfers between devices with their start and end apart: 6, of which 4 were waited for; matrix products, arithmetic and copies ran while one was open for 9% of the time, Pallas kernels for 0%

commit v1 on v0

v1 whole, which is shorter than its diff:
```python
import functools

import jax
import jax.numpy as jnp
from jax import lax
from jax.experimental import pallas as pl
from jax.experimental.pallas import tpu as pltpu
from jax.sharding import PartitionSpec as P

D = 256
HEADS = 4
HEAD_DIM = 64
BLOCK = 128
REACH = 2
LIST_LEN = 4
BLOCKS_DEV = 2
WINDOW = 2 * REACH + 1
LOG2E = 1.4426950408889634
CHUNKS = 2
OWN_MIB = 20
NEAR_MIB = 16
STREAM_MIB = 24
CROSS_MIB = 24
FINAL_MIB = 16
LANES = 128
SIDES = D // LANES
F32 = jnp.float32
BF16 = jnp.bfloat16


def shifted(block, distance):
    size = lax.axis_size("stream")
    return lax.ppermute(block, "stream", [((i - distance) % size, i) for i in range(size)])


def dot(left, right):
    return jnp.dot(left, right, preferred_element_type=F32)


def dot_t(left, right):
    return lax.dot_general(left, right, (((1,), (1,)), ((), ())), preferred_element_type=F32)


def normed_rows(values, gain_row):
    floats = values.astype(F32)
    mean = jnp.mean(floats * floats, axis=-1, keepdims=True)
    return (floats * lax.rsqrt(mean + 1e-05) * gain_row).astype(BF16)


def head_groups():
    rows = lax.broadcasted_iota(jnp.int32, (D, D), 0) // HEAD_DIM
    cols = lax.broadcasted_iota(jnp.int32, (D, D), 1) // HEAD_DIM
    return jnp.where(rows == cols, 1.0 / HEAD_DIM, 0.0).astype(BF16)


def head_factor(product, groups):
    square = product * product
    high = square.astype(BF16)
    low = (square - high.astype(F32)).astype(BF16)
    return lax.rsqrt(dot(high, groups) + dot(low, groups) + 1e-06)


def head_stack(queries):
    lane = lax.broadcasted_iota(jnp.int32, queries.shape, 1) // HEAD_DIM
    zero = jnp.zeros_like(queries)
    return jnp.concatenate([jnp.where(lane == h, queries, zero) for h in range(HEADS)], axis=0)


def attend(stack, keys, values, bias):
    scores = dot_t(stack, keys)
    if bias is not None:
        scores = scores + bias
    weights = jnp.exp2(scores)
    totals = jnp.sum(weights, axis=-1, keepdims=True)
    summed = dot(weights.astype(BF16), values) / totals
    count = stack.shape[0] // HEADS
    lane = lax.broadcasted_iota(jnp.int32, (count, D), 1) // HEAD_DIM
    result = summed[:count]
    for h in range(1, HEADS):
        result = jnp.where(lane == h, summed[h * count : (h + 1) * count], result)
    return result


def key_value(tokens, gain_row, key_weight, value_weight, groups):
    normed = normed_rows(tokens, gain_row)
    keys = dot(normed, key_weight)
    return (keys * head_factor(keys, groups)).astype(BF16), dot(normed, value_weight).astype(BF16)


def scale_row(scale_ref):
    head = lax.broadcasted_iota(jnp.int32, (1, D), 1) // HEAD_DIM
    row = jnp.zeros((1, D), F32)
    for h in range(HEADS):
        row = jnp.where(head == h, scale_ref[h] * (LOG2E / HEAD_DIM), row)
    return row


def fill_bias(order_ref, table_ref, bias_ref, per_azim):
    shape = (2 * HEAD_DIM, 2 * HEAD_DIM)
    azimuths = order_ref.shape[0]

    def placed(axis):
        row = per_azim(lax.broadcasted_iota(jnp.int32, shape, axis) % HEAD_DIM)
        found = jnp.zeros(shape, jnp.int32)
        for a in range(azimuths):
            found = jnp.where(row == a, order_ref[a], found)
        return found

    distance = placed(0) - placed(1)
    distance = jnp.where(distance < 0, distance + azimuths, distance)
    same = (lax.broadcasted_iota(jnp.int32, shape, 0) // HEAD_DIM) == (
        lax.broadcasted_iota(jnp.int32, shape, 1) // HEAD_DIM
    )
    distance = jnp.where(same, distance, -1)
    for h in range(HEADS):
        value = jnp.full(shape, -1e30, F32)
        for m in range(azimuths):
            value = jnp.where(distance == m, table_ref[h, m] * LOG2E, value)
        bias_ref[h * shape[0] : (h + 1) * shape[0]] = value


def own_kernel(
    scale_ref,
    order_ref,
    table_ref,
    field_ref,
    gain_ref,
    query_weight_ref,
    key_weight_ref,
    value_weight_ref,
    query_ref,
    kv_ref,
    bias_ref,
    *,
    per_azim,
):
    groups = head_groups()
    row = scale_row(scale_ref)
    fill_bias(order_ref, table_ref, bias_ref, per_azim)
    for line in range(field_ref.shape[0]):
        normed = normed_rows(field_ref[line], gain_ref[...])
        keys = dot(normed, key_weight_ref[...])
        kv_ref[line, :, :D] = (keys * head_factor(keys, groups)).astype(BF16)
        kv_ref[line, :, D:] = dot(normed, value_weight_ref[...]).astype(BF16)
        queries = dot(normed, query_weight_ref[...])
        query_ref[line] = (queries * head_factor(queries, groups) * row).astype(BF16)


def near_kernel(first_ref, second_ref, gain_ref, key_weight_ref, value_weight_ref, first_out, second_out):
    groups = head_groups()
    for source, target in ((first_ref, first_out), (second_ref, second_out)):
        for line in range(source.shape[0]):
            keys, values = key_value(
                source[line], gain_ref[...], key_weight_ref[...], value_weight_ref[...], groups
            )
            target[line, :, :D] = keys
            target[line, :, D:] = values


def stream_kernel(
    position_ref,
    list_ref,
    query_ref,
    field_ref,
    kv_own_ref,
    kv_next_ref,
    kv_prev_ref,
    far_next_ref,
    far_prev_ref,
    gain_ref,
    key_weight_ref,
    value_weight_ref,
    out_weight_ref,
    gain_cross_ref,
    *refs,
    first_line,
    size,
):
    after_ref, send_ref, window = refs[-3:]
    groups = head_groups()
    length = BLOCKS_DEV * BLOCK
    starts = []
    for block in range(BLOCKS_DEV):
        for j in range(LIST_LEN):
            named = list_ref[block, j]
            section = lax.rem(named // BLOCKS_DEV + REACH + size - position_ref[0], size)
            starts.append(section * length + (named % BLOCKS_DEV) * BLOCK)
    for line in range(far_next_ref.shape[0]):
        for place, source, at in (
            (1, kv_prev_ref, line),
            (2, kv_own_ref, first_line + line),
            (3, kv_next_ref, line),
        ):
            window[place * length : (place + 1) * length] = source[at]
        for place, source in ((0, far_prev_ref), (4, far_next_ref)):
            keys, values = key_value(
                source[line], gain_ref[...], key_weight_ref[...], value_weight_ref[...], groups
            )
            window[place * length : (place + 1) * length, :D] = keys
            window[place * length : (place + 1) * length, D:] = values
        parts = []
        for block in range(BLOCKS_DEV):
            stack = head_stack(query_ref[first_line + line, block * BLOCK : (block + 1) * BLOCK])
            picked = [
                window[pl.ds(pl.multiple_of(starts[block * LIST_LEN + j], BLOCK), BLOCK)]
                for j in range(LIST_LEN)
            ]
            listed = jnp.concatenate(picked, axis=0)
            parts.append(attend(stack, listed[:, :D], listed[:, D:], None))
        attended = jnp.concatenate(parts, axis=0).astype(BF16)
        fields = field_ref[first_line + line].astype(F32)
        after = (fields + dot(attended, out_weight_ref[...])).astype(BF16)
        after_ref[line] = after
        normed = normed_rows(after, gain_cross_ref[...])
        send_ref[:, first_line + line] = normed.reshape(send_ref.shape[:1] + send_ref.shape[2:])


def cross_kernel(
    scale_ref,
    source_ref,
    query_weight_ref,
    key_weight_ref,
    value_weight_ref,
    bias_ref,
    out_ref,
    gathered,
    result,
):
    groups = head_groups()
    row = scale_row(scale_ref)
    group, line_count, rows = out_ref.shape[:3]
    tokens = group * line_count
    block = source_ref[...].reshape(tokens * rows, D).astype(F32)
    for side in range(SIDES):
        gathered[side] = block[:, side * LANES : (side + 1) * LANES]
    for pair in range(rows // 2):
        both = jnp.concatenate(
            [
                jnp.concatenate(
                    [gathered[side, pl.ds(2 * pair + i, tokens, stride=rows)] for i in range(2)],
                    axis=0,
                )
                for side in range(SIDES)
            ],
            axis=1,
        ).astype(BF16)
        queries = dot(both, query_weight_ref[...])
        keys = dot(both, key_weight_ref[...])
        values = dot(both, value_weight_ref[...]).astype(BF16)
        queries = (queries * head_factor(queries, groups) * row).astype(BF16)
        keys = (keys * head_factor(keys, groups)).astype(BF16)
        attended = attend(head_stack(queries), keys, values, bias_ref[...])
        for i in range(2):
            for side in range(SIDES):
                result[side, pl.ds(2 * pair + i, tokens, stride=rows)] = attended[
                    i * tokens : (i + 1) * tokens, side * LANES : (side + 1) * LANES
                ]
    joined = jnp.concatenate([result[side] for side in range(SIDES)], axis=1)
    out_ref[...] = joined.astype(BF16).reshape(out_ref.shape)


def final_kernel(returned_ref, *refs):
    afters = refs[:CHUNKS]
    weight_ref, out_ref = refs[CHUNKS:]
    lines = out_ref.shape[0] // CHUNKS
    for line in range(out_ref.shape[0]):
        attended = returned_ref[:, line].reshape(-1, D)
        after = afters[line // lines][line % lines].astype(F32)
        out_ref[line] = (after + dot(attended, weight_ref[...])).astype(BF16)


VMEM = pl.BlockSpec(memory_space=pltpu.VMEM)
SMEM = pl.BlockSpec(memory_space=pltpu.SMEM)


def params(mib):
    return pltpu.CompilerParams(vmem_limit_bytes=mib << 20)


def cost(flops, nbytes, exps=0):
    return pl.CostEstimate(flops=flops, bytes_accessed=nbytes, transcendentals=exps)


def per_device(
    field,
    gain_stream,
    gain_cross,
    stream_query,
    stream_key,
    stream_value,
    stream_out,
    cross_query,
    cross_key,
    cross_value,
    cross_out,
    stream_scale,
    cross_scale,
    azim_bias,
    azim_order,
    block_lists,
):
    line_count = field.shape[0] * field.shape[1]
    length = field.shape[2]
    azims = lax.axis_size("azim")
    slabs = lax.axis_size("slab")
    group = azims * slabs
    rows = length // group
    lines = line_count // CHUNKS
    tokens = field.reshape(line_count, length, D)
    size = lax.axis_size("stream")

    pieces = [tokens[:lines]]
    for c in range(1, CHUNKS):
        held, _ = lax.optimization_barrier((tokens, pieces[-1]))
        pieces.append(held[c * lines : (c + 1) * lines])
    near = [(shifted(piece, 1), shifted(piece, -1)) for piece in pieces]
    far = [(shifted(ahead, 1), shifted(behind, -1)) for ahead, behind in near]

    gain_row = gain_stream.reshape(1, D)
    gain_cross_row = gain_cross.reshape(1, D)
    lines_per = field.shape[1]
    position = lax.axis_index("stream").astype(jnp.int32).reshape(1)

    def per_azim(token):
        device = token // line_count
        return (device // slabs) * field.shape[0] + (token % line_count) // lines_per

    shape = jax.ShapeDtypeStruct
    queries, kv_own, bias = pl.pallas_call(
        functools.partial(own_kernel, per_azim=per_azim),
        in_specs=[SMEM] * 3 + [VMEM] * 5,
        out_specs=[VMEM] * 3,
        out_shape=[
            shape((line_count, length, D), BF16),
            shape((line_count, length, 2 * D), BF16),
            shape((HEADS * 2 * HEAD_DIM, 2 * HEAD_DIM), F32),
        ],
        compiler_params=params(OWN_MIB),
        cost_estimate=cost(1 << 29, 1 << 21),
        name="own",
    )(stream_scale, azim_order, azim_bias, tokens, gain_row, stream_query, stream_key, stream_value)

    afters = []
    send = []
    for c in range(CHUNKS):
        kv_next, kv_prev = pl.pallas_call(
            near_kernel,
            in_specs=[VMEM] * 5,
            out_specs=[VMEM] * 2,
            out_shape=[shape((lines, length, 2 * D), BF16)] * 2,
            compiler_params=params(NEAR_MIB),
            cost_estimate=cost(1 << 28, 1 << 21),
            name="near",
        )(near[c][1], near[c][0], gain_row, stream_key, stream_value)
        after, *send = pl.pallas_call(
            functools.partial(stream_kernel, first_line=c * lines, size=size),
            in_specs=[SMEM] * 2 + [VMEM] * (12 + len(send)),
            out_specs=[VMEM] * 2,
            out_shape=[shape((lines, length, D), BF16), shape((group, line_count, rows, D), BF16)],
            input_output_aliases={14: 1} if send else {},
            scratch_shapes=[pltpu.VMEM((WINDOW * length, 2 * D), BF16)],
            compiler_params=params(STREAM_MIB),
            cost_estimate=cost(3 << 29, 1 << 22, 1 << 20),
            name="stream",
        )(
            position,
            block_lists,
            queries,
            tokens,
            kv_own,
            kv_next,
            kv_prev,
            far[c][1],
            far[c][0],
            gain_row,
            stream_key,
            stream_value,
            stream_out,
            gain_cross_row,
            *send,
        )
        afters.append(after)

    arrived = lax.all_to_all(send[0], ("azim", "slab"), 0, 0, tiled=True)
    crossed = pl.pallas_call(
        cross_kernel,
        in_specs=[SMEM] + [VMEM] * 5,
        out_specs=VMEM,
        out_shape=shape((group, line_count, rows, D), BF16),
        scratch_shapes=[pltpu.VMEM((SIDES, group * line_count * rows, LANES), F32)] * 2,
        compiler_params=params(CROSS_MIB),
        cost_estimate=cost(1 << 30, 1 << 21, 1 << 19),
        name="cross",
    )(cross_scale, arrived, cross_query, cross_key, cross_value, bias)
    returned = lax.all_to_all(crossed, ("azim", "slab"), 0, 0, tiled=True)

    result = pl.pallas_call(
        final_kernel,
        in_specs=[VMEM] * (2 + CHUNKS),
        out_specs=VMEM,
        out_shape=shape((line_count, length, D), BF16),
        compiler_params=params(FINAL_MIB),
        cost_estimate=cost(1 << 27, 3 << 19),
        name="final",
    )(returned, *afters, cross_out)
    return result.reshape(field.shape)


def solution(mesh):
    in_specs = (
        P("azim", "slab", "stream", None),
        P(),
        P(),
        P(),
        P(),
        P(),
        P(),
        P(),
        P(),
        P(),
        P(),
        P(),
        P(),
        P(),
        P(),
        P("stream", None),
    )
    out_specs = P("azim", "slab", "stream", None)
    return jax.shard_map(
        per_device, mesh=mesh, in_specs=in_specs, out_specs=out_specs, check_vma=False
    )
```

time: 186 us -> 81.5 us (0.44)
  the two profiles are of different devices: /device:TPU:32 before, /device:TPU:1 now
where the time goes in v1:
time: 81.5 us; the launch traced here: 81.3 us
  blocking collectives  35.2 us (43%)
  starting transfers between devices  19.7 us (24%)
  Pallas kernels  19.1 us (23%)
  waiting for transfers between devices  3.9 us (5%)
  local copies, waits for them, and re-layouts  3.08 us (4%)
    all_to_all x1, blocking collectives, per_device(): arrived = lax.all_to_all(send[0], ('azim', 'slab'), 0, 0, tiled=True)  20.2 us
    ppermute x8, starting transfers between devices, shifted(): lax.ppermute(block, 'stream', [((i - distance) % size, i) for i in range(...  19.7 us
    all_to_all x1, blocking collectives, per_device(): returned = lax.all_to_all(crossed, ('azim', 'slab'), 0, 0, tiled=True)  15.1 us
    pallas_call x2, Pallas kernels, per_device(): pl.pallas_call(functools.partial(stream_kernel, first_line=c * lines, siz...  7.94 us
    pallas_call x1, Pallas kernels, per_device(): pl.pallas_call(cross_kernel, in_specs=[SMEM] + [VMEM] * 5, out_specs=VMEM...  5.92 us
    ppermute x8, waiting for transfers between devices, shifted(): lax.ppermute(block, 'stream', [((i - distance) % size, i) for i in range(...  3.9 us
    pallas_call x1, Pallas kernels, per_device(): pl.pallas_call(functools.partial(own_kernel, per_azim=per_azim), in_specs...  2.38 us
    unnamed x32, local copies, waits for them, and re-layouts  2.02 us
  transfers between devices with their start and end apart: 8, of which 4 were waited for; matrix products, arithmetic and copies ran while one was open for 0% of the time, Pallas kernels for 10%

profile of v1, /device:TPU:1, one launch (start us, length us, event | category | flops | bytes accessed | tf_op | source)
XLA Modules:
  0.0 81.3 jit_solution(12266880652946960226)
XLA Ops:
  0.0 1.0 %slice_bitcast_fusion = bf16[2,256,256]{2,1,0:T(8,128)(2,1)S(1)} fusion(bf16[2,2,256,256]{3,2,1,0:T(8,128)(2,1)} %param.16), kind=kLoop, calls=%fused_computation | loop fusion | bytes 524288 | tf_op jit(solution)/shard_map/slice | solution.py:312
  1.0 7.5 %collective-permute-start.4 = (bf16[2,256,256]{2,1,0:T(8,128)(2,1)S(1)}, bf16[2,256,256]{2,1,0:T(8,128)(2,1)S(1)}, u32[]{:S(2)}, u32[]{:S(2)}) collective-permute-start(bf16[2,256,256]{2,1,0:T(8,128)(2,1)S(1)} %slice_bitcast_fusion), channel_id=1, source_target_pairs={{16,0},{32,16},{48,32},{64,48},{80,64},{96,80},{112,96},{128,112},... | collective-permute-start | bytes 786440 | tf_op jit(solution)/shard_map/ppermute | solution.py:33
  8.5 0.0 copy-start.4
  8.6 3.6 %collective-permute-start = (bf16[2,256,256]{2,1,0:T(8,128)(2,1)S(1)}, bf16[2,256,256]{2,1,0:T(8,128)(2,1)S(1)}, u32[]{:S(2)}, u32[]{:S(2)}) collective-permute-start(bf16[2,256,256]{2,1,0:T(8,128)(2,1)S(1)} %slice.11), channel_id=1, source_target_pairs={{16,0},{32,16},{48,32},{64,48},{80,64},{96,80},{112,96},{128,112},... | collective-permute-start | bytes 786440 | tf_op jit(solution)/shard_map/ppermute | solution.py:33
  12.2 1.3 %collective-permute-done.4.first_ref = bf16[2,256,256]{2,1,0:T(8,128)(2,1)S(1)} collective-permute-done((bf16[2,256,256]{2,1,0:T(8,128)(2,1)S(1)}, bf16[2,256,256]{2,1,0:T(8,128)(2,1)S(1)}, u32[]{:S(2)}, u32[]{:S(2)}) %collective-permute-start.4) | collective-permute-done | bytes 262176 | tf_op jit(solution)/shard_map/ppermute | solution.py:33
  13.5 4.3 %collective-permute-start.6 = (bf16[2,256,256]{2,1,0:T(8,128)(2,1)S(1)}, bf16[2,256,256]{2,1,0:T(8,128)(2,1)S(1)}, u32[]{:S(2)}, u32[]{:S(2)}) collective-permute-start(bf16[2,256,256]{2,1,0:T(8,128)(2,1)S(1)} %collective-permute-done.4.first_ref), channel_id=1, source_target_pairs={{16,0},{32,16},{48,32},{64,48},{80,64},{96,80},{112,96},{128,112},... | collective-permute-start | bytes 786440 | tf_op jit(solution)/shard_map/ppermute | solution.py:33
  17.8 1.3 %collective-permute-done.first_ref = bf16[2,256,256]{2,1,0:T(8,128)(2,1)S(1)} collective-permute-done((bf16[2,256,256]{2,1,0:T(8,128)(2,1)S(1)}, bf16[2,256,256]{2,1,0:T(8,128)(2,1)S(1)}, u32[]{:S(2)}, u32[]{:S(2)}) %collective-permute-start) | collective-permute-done | bytes 262176 | tf_op jit(solution)/shard_map/ppermute | solution.py:33
  19.1 4.3 %collective-permute-start.2 = (bf16[2,256,256]{2,1,0:T(8,128)(2,1)S(1)}, bf16[2,256,256]{2,1,0:T(8,128)(2,1)S(1)}, u32[]{:S(2)}, u32[]{:S(2)}) collective-permute-start(bf16[2,256,256]{2,1,0:T(8,128)(2,1)S(1)} %collective-permute-done.first_ref), channel_id=1, source_target_pairs={{16,0},{32,16},{48,32},{64,48},{80,64},{96,80},{112,96},{128,112},... | collective-permute-start | bytes 786440 | tf_op jit(solution)/shard_map/ppermute | solution.py:33
  23.5 0.0 copy-start.11
  23.5 0.6 copy-done.9
  24.1 0.0 copy-done.11
  24.2 2.4 %own.1 = (bf16[4,256,256]{2,1,0:T(8,128)(2,1)S(1)}, bf16[4,256,512]{2,1,0:T(8,128)(2,1)S(1)}, f32[512,128]{1,0:T(8,128)S(1)}) custom-call(f32[4]{0:T(128)S(1)} %copy-done.13, s32[8]{0:T(128)S(1)} %copy-done.14, f32[4,8]{1,0:T(4,128)S(1)} %copy-done.9, bf16[4,256,256]{2,1,0:T(8,128)(2,1)S(1)} %bitcast.8, f32[1,256]{1,0:T(1,128)S(1)} %bitcast.11, ...), custom_call_target="tpu_custom_call" | custom-call | flops 536870912 | bytes 2097152 | tf_op jit(solution)/shard_map/own/pallas_call | solution.py:329
  26.5 0.9 %near.3 = (bf16[2,256,512]{2,1,0:T(8,128)(2,1)S(1)}, bf16[2,256,512]{2,1,0:T(8,128)(2,1)S(1)}) custom-call(bf16[2,256,256]{2,1,0:T(8,128)(2,1)S(1)} %collective-permute-done.4.first_ref, bf16[2,256,256]{2,1,0:T(8,128)(2,1)S(1)} %collective-permute-done.5.second_ref, f32[1,256]{1,0:T(1,128)S(1)} %bitcast.12, bf16[256,256]{1,0:T(8,128)(2,1)S(1)} %copy-done.3, ...), custom_call_target="tpu_custom_call" | custom-call | flops 268435456 | bytes 2097152 | tf_op jit(solution)/shard_map/near/pallas_call | solution.py:346
  27.5 0.9 %near.2 = (bf16[2,256,512]{2,1,0:T(8,128)(2,1)S(1)}, bf16[2,256,512]{2,1,0:T(8,128)(2,1)S(1)}) custom-call(bf16[2,256,256]{2,1,0:T(8,128)(2,1)S(1)} %collective-permute-done.first_ref, bf16[2,256,256]{2,1,0:T(8,128)(2,1)S(1)} %collective-permute-done.1.second_ref, f32[1,256]{1,0:T(1,128)S(1)} %bitcast.13, bf16[256,256]{1,0:T(8,128)(2,1)S(1)} %copy-done.3, ...), custom_call_target="tpu_custom_call" | custom-call | flops 268435456 | bytes 2097152 | tf_op jit(solution)/shard_map/near/pallas_call | solution.py:346
  28.4 0.3 collective-permute-done.7.far_prev_ref
  28.7 0.7 copy-done.10
  29.4 4.0 %stream.2 = (bf16[2,256,256]{2,1,0:T(8,128)(2,1)S(1)}, bf16[16,4,16,256]{3,2,1,0:T(8,128)(2,1)S(1)}) custom-call(s32[1]{0:T(128)} %bitcast.position_ref, s32[2,4]{1,0:T(2,128)S(1)} %copy-done.10, bf16[4,256,256]{2,1,0:T(8,128)(2,1)S(1)} %get-tuple-element.17.query_ref, bf16[4,256,256]{2,1,0:T(8,128)(2,1)S(1)} %bitcast.9, ...), custom_call_target="tpu_custom_call" | custom-call | flops 1610612736 | bytes 4194304 | tf_op jit(solution)/shard_map/stream/pallas_call | solution.py:355
  33.4 1.0 %collective-permute-done.3.far_prev_ref = bf16[2,256,256]{2,1,0:T(8,128)(2,1)S(1)} collective-permute-done((bf16[2,256,256]{2,1,0:T(8,128)(2,1)S(1)}, bf16[2,256,256]{2,1,0:T(8,128)(2,1)S(1)}, u32[]{:S(2)}, u32[]{:S(2)}) %collective-permute-start.3) | collective-permute-done | bytes 262176 | tf_op jit(solution)/shard_map/ppermute | solution.py:33
  34.3 4.0 %stream.3 = (bf16[2,256,256]{2,1,0:T(8,128)(2,1)S(1)}, bf16[16,4,16,256]{3,2,1,0:T(8,128)(2,1)S(1)}) custom-call(s32[1]{0:T(128)} %bitcast.position_ref, s32[2,4]{1,0:T(2,128)S(1)} %copy-done.10, bf16[4,256,256]{2,1,0:T(8,128)(2,1)S(1)} %get-tuple-element.17.query_ref, bf16[4,256,256]{2,1,0:T(8,128)(2,1)S(1)} %bitcast.10, ...), custom_call_target="tpu_custom_call", output_to_operand_aliasing={{1}: (14, {})} | custom-call | flops 1610612736 | bytes 4194304 | tf_op jit(solution)/shard_map/stream/pallas_call | solution.py:355
  38.4 20.2 %all_to_all.10.source_ref = bf16[16,4,16,256]{3,2,1,0:T(8,128)(2,1)S(1)} all-to-all(bf16[16,4,16,256]{3,2,1,0:T(8,128)(2,1)S(1)} %get-tuple-element.25), channel_id=1, replica_groups=mesh['stream'=16,'azim'=4,'slab'=4] {'azim','slab'}, dimensions={0} | all-to-all | bytes 1048576 | tf_op jit(solution)/shard_map/all_to_all | solution.py:384
  58.5 0.6 copy-done.15
  59.2 5.9 %cross.1 = bf16[16,4,16,256]{3,2,1,0:T(8,128)(2,1)S(1)} custom-call(f32[4]{0:T(128)S(1)} %copy-done.15, bf16[16,4,16,256]{3,2,1,0:T(8,128)(2,1)S(1)} %all_to_all.10.source_ref, bf16[256,256]{1,0:T(8,128)(2,1)S(1)} %copy-done.6, bf16[256,256]{1,0:T(8,128)(2,1)S(1)} %copy-done.7, bf16[256,256]{1,0:T(8,128)(2,1)S(1)} %copy-done.8, ...), custom_call_target="tpu_custom_call" | custom-call | flops 1073741824 | bytes 2097152 | tf_op jit(solution)/shard_map/cross/pallas_call | solution.py:385
  65.1 15.1 %all_to_all.11.returned_ref = bf16[16,4,16,256]{3,2,1,0:T(8,128)(2,1)S(1)} all-to-all(bf16[16,4,16,256]{3,2,1,0:T(8,128)(2,1)S(1)} %cross.1), channel_id=1, replica_groups=mesh['stream'=16,'azim'=4,'slab'=4] {'azim','slab'}, dimensions={0} | all-to-all | bytes 1048576 | tf_op jit(solution)/shard_map/all_to_all | solution.py:395
  80.2 1.1 %final.1 = bf16[4,256,256]{2,1,0:T(8,128)(2,1)} custom-call(bf16[16,4,16,256]{3,2,1,0:T(8,128)(2,1)S(1)} %all_to_all.11.returned_ref, bf16[2,256,256]{2,1,0:T(8,128)(2,1)S(1)} %get-tuple-element.27.refs_0_, bf16[2,256,256]{2,1,0:T(8,128)(2,1)S(1)} %get-tuple-element.28.refs_1_, bf16[256,256]{1,0:T(8,128)(2,1)S(1)} %copy-done.1), custom_call_target="tpu_custom_call" | custom-call | flops 134217728 | bytes 1572864 | tf_op jit(solution)/shard_map/final/pallas_call | solution.py:397
  (35 shorter events, 0.1 us)
Async XLA Ops:
  0.0 8.5 %copy-start = (bf16[2,2,256,256]{3,2,1,0:T(8,128)(2,1)S(1)}, bf16[2,2,256,256]{3,2,1,0:T(8,128)(2,1)}, u32[]{:S(2)}) copy-start(bf16[2,2,256,256]{3,2,1,0:T(8,128)(2,1)} %param.16) | copy-start | bytes 1572868
  1.0 12.5 %collective-permute-start.4 = (bf16[2,256,256]{2,1,0:T(8,128)(2,1)S(1)}, bf16[2,256,256]{2,1,0:T(8,128)(2,1)S(1)}, u32[]{:S(2)}, u32[]{:S(2)}) collective-permute-start(bf16[2,256,256]{2,1,0:T(8,128)(2,1)S(1)} %slice_bitcast_fusion), channel_id=1, source_target_pairs={{16,0},{32,16},{48,32},{64,48},{80,64},{96,80},{112,96},{128,112},... | collective-permute-start | bytes 786440 | tf_op jit(solution)/shard_map/ppermute | solution.py:33
  8.5 9.3 %collective-permute-start.5 = (bf16[2,256,256]{2,1,0:T(8,128)(2,1)S(1)}, bf16[2,256,256]{2,1,0:T(8,128)(2,1)S(1)}, u32[]{:S(2)}, u32[]{:S(2)}) collective-permute-start(bf16[2,256,256]{2,1,0:T(8,128)(2,1)S(1)} %slice_bitcast_fusion), channel_id=1, source_target_pairs={{240,0},{0,16},{16,32},{32,48},{48,64},{64,80},{80,96},{96,112},{1... | collective-permute-start | bytes 786440 | tf_op jit(solution)/shard_map/ppermute | solution.py:33
  8.5 15.0 %copy-start.2 = (bf16[256,256]{1,0:T(8,128)(2,1)S(1)}, bf16[256,256]{1,0:T(8,128)(2,1)}, u32[]{:S(2)}) copy-start(bf16[256,256]{1,0:T(8,128)(2,1)} %query_weight_ref.2) | copy-start | bytes 393220
  8.5 15.0 %copy-start.3 = (bf16[256,256]{1,0:T(8,128)(2,1)S(1)}, bf16[256,256]{1,0:T(8,128)(2,1)}, u32[]{:S(2)}) copy-start(bf16[256,256]{1,0:T(8,128)(2,1)} %key_weight_ref.10) | copy-start | bytes 393220
  8.5 15.0 %copy-start.4 = (bf16[256,256]{1,0:T(8,128)(2,1)S(1)}, bf16[256,256]{1,0:T(8,128)(2,1)}, u32[]{:S(2)}) copy-start(bf16[256,256]{1,0:T(8,128)(2,1)} %value_weight_ref.10) | copy-start | bytes 393220
  8.6 15.0 %copy-start.14 = (s32[8]{0:T(128)S(1)}, s32[8]{0:T(128)}, u32[]{:S(2)}) copy-start(s32[8]{0:T(128)} %order_ref.1) | copy-start | bytes 100
  8.6 10.5 %collective-permute-start = (bf16[2,256,256]{2,1,0:T(8,128)(2,1)S(1)}, bf16[2,256,256]{2,1,0:T(8,128)(2,1)S(1)}, u32[]{:S(2)}, u32[]{:S(2)}) collective-permute-start(bf16[2,256,256]{2,1,0:T(8,128)(2,1)S(1)} %slice.11), channel_id=1, source_target_pairs={{16,0},{32,16},{48,32},{64,48},{80,64},{96,80},{112,96},{128,112},... | collective-permute-start | bytes 786440 | tf_op jit(solution)/shard_map/ppermute | solution.py:33
  12.2 11.2 %collective-permute-start.1 = (bf16[2,256,256]{2,1,0:T(8,128)(2,1)S(1)}, bf16[2,256,256]{2,1,0:T(8,128)(2,1)S(1)}, u32[]{:S(2)}, u32[]{:S(2)}) collective-permute-start(bf16[2,256,256]{2,1,0:T(8,128)(2,1)S(1)} %slice.11), channel_id=1, source_target_pairs={{240,0},{0,16},{16,32},{32,48},{48,64},{64,80},{80,96},{96,112},{1... | collective-permute-start | bytes 786440 | tf_op jit(solution)/shard_map/ppermute | solution.py:33
  13.5 14.9 %collective-permute-start.6 = (bf16[2,256,256]{2,1,0:T(8,128)(2,1)S(1)}, bf16[2,256,256]{2,1,0:T(8,128)(2,1)S(1)}, u32[]{:S(2)}, u32[]{:S(2)}) collective-permute-start(bf16[2,256,256]{2,1,0:T(8,128)(2,1)S(1)} %collective-permute-done.4.first_ref), channel_id=1, source_target_pairs={{16,0},{32,16},{48,32},{64,48},{80,64},{96,80},{112,96},{128,112},... | collective-permute-start | bytes 786440 | tf_op jit(solution)/shard_map/ppermute | solution.py:33
  17.8 10.9 %collective-permute-start.7 = (bf16[2,256,256]{2,1,0:T(8,128)(2,1)S(1)}, bf16[2,256,256]{2,1,0:T(8,128)(2,1)S(1)}, u32[]{:S(2)}, u32[]{:S(2)}) collective-permute-start(bf16[2,256,256]{2,1,0:T(8,128)(2,1)S(1)} %collective-permute-done.5.second_ref), channel_id=1, source_target_pairs={{240,0},{0,16},{16,32},{32,48},{48,64},{64,80},{80,96},{96,112},{1... | collective-permute-start | bytes 786440 | tf_op jit(solution)/shard_map/ppermute | solution.py:33
  19.1 14.2 %collective-permute-start.2 = (bf16[2,256,256]{2,1,0:T(8,128)(2,1)S(1)}, bf16[2,256,256]{2,1,0:T(8,128)(2,1)S(1)}, u32[]{:S(2)}, u32[]{:S(2)}) collective-permute-start(bf16[2,256,256]{2,1,0:T(8,128)(2,1)S(1)} %collective-permute-done.first_ref), channel_id=1, source_target_pairs={{16,0},{32,16},{48,32},{64,48},{80,64},{96,80},{112,96},{128,112},... | collective-permute-start | bytes 786440 | tf_op jit(solution)/shard_map/ppermute | solution.py:33
  23.4 10.9 %collective-permute-start.3 = (bf16[2,256,256]{2,1,0:T(8,128)(2,1)S(1)}, bf16[2,256,256]{2,1,0:T(8,128)(2,1)S(1)}, u32[]{:S(2)}, u32[]{:S(2)}) collective-permute-start(bf16[2,256,256]{2,1,0:T(8,128)(2,1)S(1)} %collective-permute-done.1.second_ref), channel_id=1, source_target_pairs={{240,0},{0,16},{16,32},{32,48},{48,64},{64,80},{80,96},{96,112},{1... | collective-permute-start | bytes 786440 | tf_op jit(solution)/shard_map/ppermute | solution.py:33
  23.5 0.7 copy-start.9
  23.5 0.7 copy-start.11
  23.5 0.7 copy-start.13
  27.4 1.3 %copy-start.5 = (bf16[256,256]{1,0:T(8,128)(2,1)S(1)}, bf16[256,256]{1,0:T(8,128)(2,1)}, u32[]{:S(2)}) copy-start(bf16[256,256]{1,0:T(8,128)(2,1)} %out_weight_ref.3) | copy-start | bytes 393220
  27.5 1.3 %copy-start.12 = (f32[256]{0:T(256)S(1)}, f32[256]{0:T(256)}, u32[]{:S(2)}) copy-start(f32[256]{0:T(256)} %param.18) | copy-start | bytes 3076
  28.7 0.7 copy-start.10
  38.3 20.2 %copy-start.6 = (bf16[256,256]{1,0:T(8,128)(2,1)S(1)}, bf16[256,256]{1,0:T(8,128)(2,1)}, u32[]{:S(2)}) copy-start(bf16[256,256]{1,0:T(8,128)(2,1)} %query_weight_ref.3) | copy-start | bytes 393220
  38.3 20.2 %copy-start.7 = (bf16[256,256]{1,0:T(8,128)(2,1)S(1)}, bf16[256,256]{1,0:T(8,128)(2,1)}, u32[]{:S(2)}) copy-start(bf16[256,256]{1,0:T(8,128)(2,1)} %key_weight_ref.11) | copy-start | bytes 393220
  38.4 20.2 %copy-start.8 = (bf16[256,256]{1,0:T(8,128)(2,1)S(1)}, bf16[256,256]{1,0:T(8,128)(2,1)}, u32[]{:S(2)}) copy-start(bf16[256,256]{1,0:T(8,128)(2,1)} %value_weight_ref.11) | copy-start | bytes 393220
  58.5 0.7 copy-start.15
  65.1 15.1 %copy-start.1 = (bf16[256,256]{1,0:T(8,128)(2,1)S(1)}, bf16[256,256]{1,0:T(8,128)(2,1)}, u32[]{:S(2)}) copy-start(bf16[256,256]{1,0:T(8,128)(2,1)} %refs_2_.1) | copy-start | bytes 393220

commit v2 on v1

v2 whole, which is shorter than its diff:
```python
import functools

import jax
import jax.numpy as jnp
from jax import lax
from jax.experimental import pallas as pl
from jax.experimental.pallas import tpu as pltpu
from jax.sharding import PartitionSpec as P

D = 256
HEADS = 4
HEAD_DIM = 64
BLOCK = 128
REACH = 2
LIST_LEN = 4
BLOCKS_DEV = 2
WINDOW = 2 * REACH + 1
LOG2E = 1.4426950408889634
CHUNKS = 2
FETCHED = 7
OWN_MIB = 20
NEAR_MIB = 16
STREAM_MIB = 24
CROSS_MIB = 24
FINAL_MIB = 16
LANES = 128
SIDES = D // LANES
F32 = jnp.float32
BF16 = jnp.bfloat16


def shifted(block, distance):
    size = lax.axis_size("stream")
    return lax.ppermute(block, "stream", [((i - distance) % size, i) for i in range(size)])


def dot(left, right):
    return jnp.dot(left, right, preferred_element_type=F32)


def dot_t(left, right):
    return lax.dot_general(left, right, (((1,), (1,)), ((), ())), preferred_element_type=F32)


def normed_rows(values, gain_row):
    floats = values.astype(F32)
    mean = jnp.mean(floats * floats, axis=-1, keepdims=True)
    return (floats * lax.rsqrt(mean + 1e-05) * gain_row).astype(BF16)


def head_groups():
    rows = lax.broadcasted_iota(jnp.int32, (D, D), 0) // HEAD_DIM
    cols = lax.broadcasted_iota(jnp.int32, (D, D), 1) // HEAD_DIM
    return jnp.where(rows == cols, 1.0 / HEAD_DIM, 0.0).astype(BF16)


def head_units(product, groups):
    means = dot((product * product).astype(BF16), groups)
    return product * lax.rsqrt(means + 1e-06)


def head_stack(queries):
    lane = lax.broadcasted_iota(jnp.int32, queries.shape, 1) // HEAD_DIM
    zero = jnp.zeros_like(queries)
    return jnp.concatenate([jnp.where(lane == h, queries, zero) for h in range(HEADS)], axis=0)


def attend(stack, keys, values, bias):
    scores = dot_t(stack, keys)
    if bias is not None:
        scores = scores + bias
    weights = jnp.exp2(scores)
    factors = 1.0 / jnp.sum(weights, axis=-1, keepdims=True)
    summed = dot(weights.astype(BF16), values)
    count = stack.shape[0] // HEADS
    lane = lax.broadcasted_iota(jnp.int32, (count, D), 1) // HEAD_DIM
    result = summed[:count]
    factor = jnp.broadcast_to(factors[:count], (count, D))
    for h in range(1, HEADS):
        at = slice(h * count, (h + 1) * count)
        result = jnp.where(lane == h, summed[at], result)
        factor = jnp.where(lane == h, factors[at], factor)
    return result * factor


def scale_row(scale_ref):
    head = lax.broadcasted_iota(jnp.int32, (1, D), 1) // HEAD_DIM
    row = jnp.zeros((1, D), F32)
    for h in range(HEADS):
        row = jnp.where(head == h, scale_ref[h] * (LOG2E / HEAD_DIM), row)
    return row


def prepare_kernel(position_ref, *refs, per_azim, size):
    small, fetched, refs = refs[:5], refs[5 : 5 + FETCHED], refs[5 + FETCHED :]
    stream_row_ref, cross_row_ref, start_ref, bias_ref = refs[:4]
    held, refs = refs[4 : 4 + FETCHED], refs[4 + FETCHED :]
    stream_scale_ref, cross_scale_ref, order_ref, table_ref, list_ref, sems = refs
    copies = [
        pltpu.make_async_copy(source, target, sems.at[i])
        for i, (source, target) in enumerate(zip(small + fetched, refs[:5] + held))
    ]
    for copy in copies:
        copy.start()
    for copy in copies[:5]:
        copy.wait()
    stream_row_ref[...] = scale_row(stream_scale_ref)
    cross_row_ref[...] = scale_row(cross_scale_ref)
    for block in range(BLOCKS_DEV):
        for j in range(LIST_LEN):
            named = list_ref[block, j]
            section = lax.rem(named // BLOCKS_DEV + (REACH + size) - position_ref[0], size)
            start_ref[block, j] = section * (BLOCKS_DEV * BLOCK) + (named % BLOCKS_DEV) * BLOCK
    shape = (2 * HEAD_DIM, 2 * HEAD_DIM)
    azimuths = order_ref.shape[0]

    def placed(axis):
        dims = (shape[0], 1) if axis == 0 else (1, shape[1])
        row = per_azim(lax.broadcasted_iota(jnp.int32, dims, axis) % HEAD_DIM)
        found = jnp.zeros(dims, jnp.int32)
        for a in range(azimuths):
            found = jnp.where(row == a, order_ref[a], found)
        return found

    distance = placed(0) - placed(1)
    distance = jnp.where(distance < 0, distance + azimuths, distance)
    same = (lax.broadcasted_iota(jnp.int32, shape, 0) // HEAD_DIM) == (
        lax.broadcasted_iota(jnp.int32, shape, 1) // HEAD_DIM
    )
    distance = jnp.where(same, distance, -1)
    for h in range(HEADS):
        value = jnp.full(shape, -1e30, F32)
        for m in range(azimuths):
            value = jnp.where(distance == m, table_ref[h, m] * LOG2E, value)
        bias_ref[h * shape[0] : (h + 1) * shape[0]] = value
    for copy in copies[5:]:
        copy.wait()


def own_kernel(row_ref, field_ref, gain_ref, query_weight_ref, key_weight_ref, value_weight_ref, query_ref, kv_ref):
    lines, length = field_ref.shape[:2]
    groups = head_groups()
    normed = normed_rows(field_ref[...].reshape(-1, D), gain_ref[...])
    keys = head_units(dot(normed, key_weight_ref[...]), groups).astype(BF16)
    kv_ref[:, :, :D] = keys.reshape(lines, length, D)
    queries = head_units(dot(normed, query_weight_ref[...]), groups) * row_ref[...]
    query_ref[...] = queries.astype(BF16).reshape(lines, length, D)
    kv_ref[:, :, D:] = dot(normed, value_weight_ref[...]).astype(BF16).reshape(lines, length, D)


def near_kernel(prev_ref, next_ref, own_ref, gain_ref, key_weight_ref, value_weight_ref, out_ref, *, first_line):
    lines, length = prev_ref.shape[:2]
    groups = head_groups()
    tokens = jnp.concatenate([prev_ref[...].reshape(-1, D), next_ref[...].reshape(-1, D)], axis=0)
    normed = normed_rows(tokens, gain_ref[...])
    keys = head_units(dot(normed, key_weight_ref[...]), groups).astype(BF16)
    values = dot(normed, value_weight_ref[...]).astype(BF16)
    half = lines * length
    for part, place in ((0, 0), (1, 2)):
        at = slice(place * length, (place + 1) * length)
        out_ref[:, at, :D] = keys[part * half : (part + 1) * half].reshape(lines, length, D)
        out_ref[:, at, D:] = values[part * half : (part + 1) * half].reshape(lines, length, D)
    out_ref[:, length : 2 * length] = own_ref[first_line : first_line + lines]


def stream_kernel(
    start_ref,
    query_ref,
    field_ref,
    window_ref,
    far_prev_ref,
    far_next_ref,
    gain_ref,
    key_weight_ref,
    value_weight_ref,
    out_weight_ref,
    gain_cross_ref,
    *refs,
    first_line,
):
    after_ref, send_ref, far = refs[-3:]
    earlier = refs[:-3]
    lines, length = far_prev_ref.shape[:2]
    groups = head_groups()
    tokens = jnp.concatenate(
        [far_prev_ref[...].reshape(-1, D), far_next_ref[...].reshape(-1, D)], axis=0
    )
    normed = normed_rows(tokens, gain_ref[...])
    far[:, :D] = head_units(dot(normed, key_weight_ref[...]), groups).astype(BF16)
    far[:, D:] = dot(normed, value_weight_ref[...]).astype(BF16)
    near_rows = window_ref.shape[1]
    parts = []
    for line in range(lines):
        for block in range(BLOCKS_DEV):
            stack = head_stack(query_ref[first_line + line, block * BLOCK : (block + 1) * BLOCK])
            picked = []
            for j in range(LIST_LEN):
                start = start_ref[block, j]
                before = start < length
                after = start >= length + near_rows
                near_at = jnp.where(before | after, 0, start - length)
                far_at = line * length + jnp.where(
                    before, start, jnp.where(after, start - (length + near_rows) + lines * length, 0)
                )
                close = window_ref[line, pl.ds(pl.multiple_of(near_at, BLOCK), BLOCK)]
                distant = far[pl.ds(pl.multiple_of(far_at, BLOCK), BLOCK)]
                picked.append(jnp.where(before | after, distant, close))
            listed = jnp.concatenate(picked, axis=0)
            parts.append(attend(stack, listed[:, :D], listed[:, D:], None))
    attended = jnp.concatenate(parts, axis=0).astype(BF16)
    fields = field_ref[first_line : first_line + lines].reshape(-1, D).astype(F32)
    after = (fields + dot(attended, out_weight_ref[...])).astype(BF16)
    after_ref[...] = after.reshape(lines, length, D)
    normed = normed_rows(after, gain_cross_ref[...])
    group, _, rows, _ = send_ref.shape
    for line in range(lines):
        send_ref[:, first_line + line] = normed[line * length : (line + 1) * length].reshape(
            group, rows, D
        )
    for previous in earlier:
        send_ref[:, :first_line] = previous[:, :first_line]


def cross_kernel(
    row_ref,
    source_ref,
    query_weight_ref,
    key_weight_ref,
    value_weight_ref,
    bias_ref,
    out_ref,
    mixed,
    ordered,
    query_buffer,
    key_buffer,
    value_buffer,
):
    groups = head_groups()
    group, line_count, rows = out_ref.shape[:3]
    tokens = group * line_count
    block = source_ref[...].reshape(tokens * rows, D).astype(F32)
    for side in range(SIDES):
        mixed[side] = block[:, side * LANES : (side + 1) * LANES]
    for index in range(rows):
        at = slice(index * tokens, (index + 1) * tokens)
        ordered[at] = jnp.concatenate(
            [mixed[side, pl.ds(index, tokens, stride=rows)] for side in range(SIDES)], axis=1
        ).astype(BF16)
    normed = ordered[...]
    key_buffer[...] = head_units(dot(normed, key_weight_ref[...]), groups).astype(BF16)
    query_buffer[...] = (
        head_units(dot(normed, query_weight_ref[...]), groups) * row_ref[...]
    ).astype(BF16)
    value_buffer[...] = dot(normed, value_weight_ref[...]).astype(BF16)
    for pair in range(rows // 2):
        at = slice(2 * pair * tokens, (2 * pair + 2) * tokens)
        attended = attend(
            head_stack(query_buffer[at]), key_buffer[at], value_buffer[at], bias_ref[...]
        )
        for i in range(2):
            for side in range(SIDES):
                mixed[side, pl.ds(2 * pair + i, tokens, stride=rows)] = attended[
                    i * tokens : (i + 1) * tokens, side * LANES : (side + 1) * LANES
                ]
    joined = jnp.concatenate([mixed[side] for side in range(SIDES)], axis=1)
    out_ref[...] = joined.astype(BF16).reshape(out_ref.shape)


def final_kernel(returned_ref, *refs):
    afters = refs[:CHUNKS]
    weight_ref, out_ref = refs[CHUNKS:]
    line_count, length = out_ref.shape[:2]
    lines = line_count // CHUNKS
    attended = jnp.concatenate(
        [returned_ref[:, line].reshape(-1, D) for line in range(line_count)], axis=0
    )
    after = jnp.concatenate([part[...].reshape(-1, D) for part in afters], axis=0).astype(F32)
    out_ref[...] = (after + dot(attended, weight_ref[...])).astype(BF16).reshape(out_ref.shape)


VMEM = pl.BlockSpec(memory_space=pltpu.VMEM)
SMEM = pl.BlockSpec(memory_space=pltpu.SMEM)


def params(mib):
    return pltpu.CompilerParams(vmem_limit_bytes=mib << 20)


def cost(flops, nbytes, exps=0):
    return pl.CostEstimate(flops=flops, bytes_accessed=nbytes, transcendentals=exps)


def per_device(
    field,
    gain_stream,
    gain_cross,
    stream_query,
    stream_key,
    stream_value,
    stream_out,
    cross_query,
    cross_key,
    cross_value,
    cross_out,
    stream_scale,
    cross_scale,
    azim_bias,
    azim_order,
    block_lists,
):
    line_count = field.shape[0] * field.shape[1]
    length = field.shape[2]
    azims = lax.axis_size("azim")
    slabs = lax.axis_size("slab")
    group = azims * slabs
    rows = length // group
    lines = line_count // CHUNKS
    tokens = field.reshape(line_count, length, D)
    size = lax.axis_size("stream")

    pieces = [tokens[:lines]]
    for c in range(1, CHUNKS):
        held, _ = lax.optimization_barrier((tokens, pieces[-1]))
        pieces.append(held[c * lines : (c + 1) * lines])
    near = [(shifted(piece, 1), shifted(piece, -1)) for piece in pieces]

    gain_row = gain_stream.reshape(1, D)
    gain_cross_row = gain_cross.reshape(1, D)
    lines_per = field.shape[1]
    position = lax.axis_index("stream").astype(jnp.int32).reshape(1)

    def per_azim(token):
        device = token // line_count
        return (device // slabs) * field.shape[0] + (token % line_count) // lines_per

    shape = jax.ShapeDtypeStruct
    small = [stream_scale, cross_scale, azim_order, azim_bias, block_lists]
    fetched = [tokens, gain_row, gain_cross_row, stream_query, stream_key, stream_value, stream_out]
    stream_row, cross_row, starts, bias, *held = pl.pallas_call(
        functools.partial(prepare_kernel, per_azim=per_azim, size=size),
        in_specs=[SMEM] + [pl.BlockSpec(memory_space=pltpu.HBM)] * (5 + FETCHED),
        out_specs=[VMEM, VMEM, SMEM, VMEM] + [VMEM] * FETCHED,
        out_shape=[
            shape((1, D), F32),
            shape((1, D), F32),
            shape(block_lists.shape, jnp.int32),
            shape((HEADS * 2 * HEAD_DIM, 2 * HEAD_DIM), F32),
        ]
        + [shape(array.shape, array.dtype) for array in fetched],
        scratch_shapes=[pltpu.SMEM(array.shape, array.dtype) for array in small]
        + [pltpu.SemaphoreType.DMA((5 + FETCHED,))],
        compiler_params=params(NEAR_MIB),
        cost_estimate=cost(1 << 20, 1 << 18),
        name="prepare",
    )(position, *[pltpu.with_memory_space_constraint(array, pltpu.HBM) for array in small + fetched])
    tokens, gain_row, gain_cross_row, stream_query, stream_key, stream_value, stream_out = held

    far = []
    for c, (ahead, behind) in enumerate(near):
        if c == 0:
            ahead, behind, _ = lax.optimization_barrier((ahead, behind, cross_row))
        far.append((shifted(ahead, 1), shifted(behind, -1)))

    queries, kv_own = pl.pallas_call(
        own_kernel,
        in_specs=[VMEM] * 6,
        out_specs=[VMEM] * 2,
        out_shape=[
            shape((line_count, length, D), BF16),
            shape((line_count, length, 2 * D), BF16),
        ],
        compiler_params=params(OWN_MIB),
        cost_estimate=cost(1 << 29, 1 << 21),
        name="own",
    )(stream_row, tokens, gain_row, stream_query, stream_key, stream_value)

    afters = []
    send = []
    for c in range(CHUNKS):
        window = pl.pallas_call(
            functools.partial(near_kernel, first_line=c * lines),
            in_specs=[VMEM] * 6,
            out_specs=VMEM,
            out_shape=shape((lines, 3 * length, 2 * D), BF16),
            compiler_params=params(NEAR_MIB),
            cost_estimate=cost(1 << 28, 1 << 21),
            name="near",
        )(near[c][0], near[c][1], kv_own, gain_row, stream_key, stream_value)
        after, *send = pl.pallas_call(
            functools.partial(stream_kernel, first_line=c * lines),
            in_specs=[SMEM] + [VMEM] * (10 + len(send)),
            out_specs=[VMEM] * 2,
            out_shape=[shape((lines, length, D), BF16), shape((group, line_count, rows, D), BF16)],
            scratch_shapes=[pltpu.VMEM((2 * lines * length, 2 * D), BF16)],
            compiler_params=params(STREAM_MIB),
            cost_estimate=cost(3 << 29, 1 << 22, 1 << 20),
            name="stream",
        )(
            starts,
            queries,
            tokens,
            window,
            far[c][0],
            far[c][1],
            gain_row,
            stream_key,
            stream_value,
            stream_out,
            gain_cross_row,
            *send,
        )
        afters.append(after)

    arrived = lax.all_to_all(send[0], ("azim", "slab"), 0, 0, tiled=True)
    crossed = pl.pallas_call(
        cross_kernel,
        in_specs=[VMEM] * 6,
        out_specs=VMEM,
        out_shape=shape((group, line_count, rows, D), BF16),
        scratch_shapes=[pltpu.VMEM((SIDES, group * line_count * rows, LANES), F32)]
        + [pltpu.VMEM((group * line_count * rows, D), BF16)] * 4,
        compiler_params=params(CROSS_MIB),
        cost_estimate=cost(1 << 30, 1 << 21, 1 << 19),
        name="cross",
    )(cross_row, arrived, cross_query, cross_key, cross_value, bias)
    returned = lax.all_to_all(crossed, ("azim", "slab"), 0, 0, tiled=True)

    result = pl.pallas_call(
        final_kernel,
        in_specs=[VMEM] * (2 + CHUNKS),
        out_specs=VMEM,
        out_shape=shape((line_count, length, D), BF16),
        compiler_params=params(FINAL_MIB),
        cost_estimate=cost(1 << 27, 3 << 19),
        name="final",
    )(returned, *afters, cross_out)
    return result.reshape(field.shape)


def solution(mesh):
    in_specs = (
        P("azim", "slab", "stream", None),
        P(),
        P(),
        P(),
        P(),
        P(),
        P(),
        P(),
        P(),
        P(),
        P(),
        P(),
        P(),
        P(),
        P(),
        P("stream", None),
    )
    out_specs = P("azim", "slab", "stream", None)
    return jax.shard_map(
        per_device, mesh=mesh, in_specs=in_specs, out_specs=out_specs, check_vma=False
    )
```

time: 81.5 us -> 72.2 us (0.89)
  Pallas kernels: 19.1 us -> 13.9 us
  starting transfers between devices: 19.7 us -> 18.4 us
  blocking collectives: 35.2 us -> 34 us
  local copies, waits for them, and re-layouts: 3.08 us -> 1.95 us
    pallas_call x6 -> x7, Pallas kernels: 18 us -> 12.8 us  [the longest x2 5.86 us: per_device(): pl.pallas_call(functools.partial(stream_kernel, first_line=c * lines), in...]
    unnamed x32 -> x8, local copies, waits for them, and re-layouts: 2.02 us -> 0.02 us
    ppermute x8, starting transfers between devices: 19.7 us -> 18.4 us  [shifted(): lax.ppermute(block, 'stream', [((i - distance) % size, i) for i in range(...]
    all_to_all x1, blocking collectives: 20.2 us -> 19.1 us  [per_device(): arrived = lax.all_to_all(send[0], ('azim', 'slab'), 0, 0, tiled=True)]
    slice x1, local copies, waits for them, and re-layouts: 0.02 us -> 0.97 us  [per_device(): pieces.append(held[c * lines:(c + 1) * lines])]
  transfers between devices with their start and end apart: 8 -> 8, of which waited for: 4 -> 2; matrix products, arithmetic and copies ran while one was open for 0% -> 1% of each run, Pallas kernels for 10% -> 10%
where the time goes in v2:
time: 72.2 us; the launch traced here: 71.9 us
  blocking collectives  34 us (47%)
  starting transfers between devices  18.4 us (25%)
  Pallas kernels  13.9 us (19%)
  waiting for transfers between devices  3.49 us (5%)
  local copies, waits for them, and re-layouts  1.95 us (3%)
    all_to_all x1, blocking collectives, per_device(): arrived = lax.all_to_all(send[0], ('azim', 'slab'), 0, 0, tiled=True)  19.1 us
    ppermute x8, starting transfers between devices, shifted(): lax.ppermute(block, 'stream', [((i - distance) % size, i) for i in range(...  18.4 us
    all_to_all x1, blocking collectives, per_device(): returned = lax.all_to_all(crossed, ('azim', 'slab'), 0, 0, tiled=True)  14.9 us
    pallas_call x2, Pallas kernels, per_device(): pl.pallas_call(functools.partial(stream_kernel, first_line=c * lines), in...  5.86 us
    ppermute x8, waiting for transfers between devices, shifted(): lax.ppermute(block, 'stream', [((i - distance) % size, i) for i in range(...  3.49 us
    pallas_call x1, Pallas kernels, per_device(): pl.pallas_call(cross_kernel, in_specs=[VMEM] * 6, out_specs=VMEM, out_sha...  2.73 us
    pallas_call x1, Pallas kernels, per_device(): pl.pallas_call(functools.partial(prepare_kernel, per_azim=per_azim, size=...  1.92 us
  transfers between devices with their start and end apart: 8, of which 2 were waited for; matrix products, arithmetic and copies ran while one was open for 1% of the time, Pallas kernels for 10%

profile of v2, /device:TPU:1, one launch (start us, length us, event | category | flops | bytes accessed | tf_op | source)
XLA Modules:
  0.0 71.9 jit_solution(3647597214570617405)
XLA Ops:
  0.0 1.0 %slice_bitcast_fusion = bf16[2,256,256]{2,1,0:T(8,128)(2,1)S(1)} fusion(bf16[2,2,256,256]{3,2,1,0:T(8,128)(2,1)} %param.16), kind=kLoop, calls=%fused_computation | loop fusion | bytes 524288 | tf_op jit(solution)/shard_map/slice | solution.py:321
  1.0 2.5 %collective-permute-start.4 = (bf16[2,256,256]{2,1,0:T(8,128)(2,1)S(1)}, bf16[2,256,256]{2,1,0:T(8,128)(2,1)S(1)}, u32[]{:S(2)}, u32[]{:S(2)}) collective-permute-start(bf16[2,256,256]{2,1,0:T(8,128)(2,1)S(1)} %slice_bitcast_fusion), channel_id=1, source_target_pairs={{240,0},{0,16},{16,32},{32,48},{48,64},{64,80},{80,96},{96,112},{1... | collective-permute-start | bytes 786440 | tf_op jit(solution)/shard_map/ppermute | solution.py:34
  3.5 5.0 %collective-permute-start.5 = (bf16[2,256,256]{2,1,0:T(8,128)(2,1)S(1)}, bf16[2,256,256]{2,1,0:T(8,128)(2,1)S(1)}, u32[]{:S(2)}, u32[]{:S(2)}) collective-permute-start(bf16[2,256,256]{2,1,0:T(8,128)(2,1)S(1)} %slice_bitcast_fusion), channel_id=1, source_target_pairs={{16,0},{32,16},{48,32},{64,48},{80,64},{96,80},{112,96},{128,112},... | collective-permute-start | bytes 786440 | tf_op jit(solution)/shard_map/ppermute | solution.py:34
  8.5 1.0 %slice.11 = bf16[2,256,256]{2,1,0:T(8,128)(2,1)S(1)} slice(bf16[4,256,256]{2,1,0:T(8,128)(2,1)} %bitcast.7), slice={[2:4], [0:256], [0:256]} | slice | bytes 524288 | tf_op jit(solution)/shard_map/slice | solution.py:324
  9.5 0.1 collective-permute-start
  9.6 3.6 %collective-permute-start.1 = (bf16[2,256,256]{2,1,0:T(8,128)(2,1)S(1)}, bf16[2,256,256]{2,1,0:T(8,128)(2,1)S(1)}, u32[]{:S(2)}, u32[]{:S(2)}) collective-permute-start(bf16[2,256,256]{2,1,0:T(8,128)(2,1)S(1)} %slice.11), channel_id=1, source_target_pairs={{16,0},{32,16},{48,32},{64,48},{80,64},{96,80},{112,96},{128,112},... | collective-permute-start | bytes 786440 | tf_op jit(solution)/shard_map/ppermute | solution.py:34
  13.2 1.9 %prepare.1 = (f32[1,256]{1,0:T(1,128)S(1)}, f32[1,256]{1,0:T(1,128)S(1)}, s32[2,4]{1,0:T(2,128)S(1)}, f32[512,128]{1,0:T(8,128)S(1)}, bf16[4,256,256]{2,1,0:T(8,...) custom-call(s32[1]{0:T(128)} %bitcast.position_ref, ...), custom_call_target="tpu_custom_call" | custom-call | flops 1048576 | bytes 262144 | tf_op jit(solution)/shard_map/prepare/pallas_call | solution.py:339
  15.1 0.0 collective-permute-done.4.prev_ref
  15.1 0.1 collective-permute-start.6
  15.2 3.6 %collective-permute-start.7 = (bf16[2,256,256]{2,1,0:T(8,128)(2,1)S(1)}, bf16[2,256,256]{2,1,0:T(8,128)(2,1)S(1)}, u32[]{:S(2)}, u32[]{:S(2)}) collective-permute-start(bf16[2,256,256]{2,1,0:T(8,128)(2,1)S(1)} %collective-permute-done.5.next_ref), channel_id=1, source_target_pairs={{16,0},{32,16},{48,32},{64,48},{80,64},{96,80},{112,96},{128,112},... | collective-permute-start | bytes 786440 | tf_op jit(solution)/shard_map/ppermute | solution.py:34
  18.8 1.3 %collective-permute-done.prev_ref = bf16[2,256,256]{2,1,0:T(8,128)(2,1)S(1)} collective-permute-done((bf16[2,256,256]{2,1,0:T(8,128)(2,1)S(1)}, bf16[2,256,256]{2,1,0:T(8,128)(2,1)S(1)}, u32[]{:S(2)}, u32[]{:S(2)}) %collective-permute-start) | collective-permute-done | bytes 262176 | tf_op jit(solution)/shard_map/ppermute | solution.py:34
  20.1 3.6 %collective-permute-start.3 = (bf16[2,256,256]{2,1,0:T(8,128)(2,1)S(1)}, bf16[2,256,256]{2,1,0:T(8,128)(2,1)S(1)}, u32[]{:S(2)}, u32[]{:S(2)}) collective-permute-start(bf16[2,256,256]{2,1,0:T(8,128)(2,1)S(1)} %collective-permute-done.1.next_ref), channel_id=1, source_target_pairs={{16,0},{32,16},{48,32},{64,48},{80,64},{96,80},{112,96},{128,112},... | collective-permute-start | bytes 786440 | tf_op jit(solution)/shard_map/ppermute | solution.py:34
  23.7 1.0 %own.1 = (bf16[4,256,256]{2,1,0:T(8,128)(2,1)S(1)}, bf16[4,256,512]{2,1,0:T(8,128)(2,1)S(1)}) custom-call(f32[1,256]{1,0:T(1,128)S(1)} %get-tuple-element.27.row_ref, bf16[4,256,256]{2,1,0:T(8,128)(2,1)S(1)} %get-tuple-element.28.field_ref, f32[1,256]{1,0:T(1,128)S(1)} %get-tuple-element.29.gain_ref, ...), custom_call_target="tpu_custom_call" | custom-call | flops 536870912 | bytes 2097152 | tf_op jit(solution)/shard_map/own/pallas_call | solution.py:364
  24.6 0.7 near.3.window_ref
  25.3 0.7 near.2.window_ref
  26.0 2.9 %stream.2 = (bf16[2,256,256]{2,1,0:T(8,128)(2,1)S(1)}, bf16[16,4,16,256]{3,2,1,0:T(8,128)(2,1)S(1)}) custom-call(s32[2,4]{1,0:T(2,128)S(1)} %get-tuple-element.26.start_ref, bf16[4,256,256]{2,1,0:T(8,128)(2,1)S(1)} %get-tuple-element.33.query_ref, bf16[4,256,256]{2,1,0:T(8,128)(2,1)S(1)} %get-tuple-element.28.field_ref, ...), custom_call_target="tpu_custom_call" | custom-call | flops 1610612736 | bytes 4194304 | tf_op jit(solution)/shard_map/stream/pallas_call | solution.py:389
  29.0 2.2 %collective-permute-done.2.far_prev_ref = bf16[2,256,256]{2,1,0:T(8,128)(2,1)S(1)} collective-permute-done((bf16[2,256,256]{2,1,0:T(8,128)(2,1)S(1)}, bf16[2,256,256]{2,1,0:T(8,128)(2,1)S(1)}, u32[]{:S(2)}, u32[]{:S(2)}) %collective-permute-start.2) | collective-permute-done | bytes 262176 | tf_op jit(solution)/shard_map/ppermute | solution.py:34
  31.1 0.0 collective-permute-done.3.far_next_ref
  31.1 2.9 %stream.3 = (bf16[2,256,256]{2,1,0:T(8,128)(2,1)S(1)}, bf16[16,4,16,256]{3,2,1,0:T(8,128)(2,1)S(1)}) custom-call(s32[2,4]{1,0:T(2,128)S(1)} %get-tuple-element.26.start_ref, bf16[4,256,256]{2,1,0:T(8,128)(2,1)S(1)} %get-tuple-element.33.query_ref, bf16[4,256,256]{2,1,0:T(8,128)(2,1)S(1)} %get-tuple-element.28.field_ref, ...), custom_call_target="tpu_custom_call" | custom-call | flops 1610612736 | bytes 4194304 | tf_op jit(solution)/shard_map/stream/pallas_call | solution.py:389
  34.1 19.1 %all_to_all.10.source_ref = bf16[16,4,16,256]{3,2,1,0:T(8,128)(2,1)S(1)} all-to-all(bf16[16,4,16,256]{3,2,1,0:T(8,128)(2,1)S(1)} %get-tuple-element.41), channel_id=1, replica_groups=mesh['stream'=16,'azim'=4,'slab'=4] {'azim','slab'}, dimensions={0} | all-to-all | bytes 1048576 | tf_op jit(solution)/shard_map/all_to_all | solution.py:414
  53.2 0.0 copy-start
  53.2 2.7 %cross.1 = bf16[16,4,16,256]{3,2,1,0:T(8,128)(2,1)S(1)} custom-call(f32[1,256]{1,0:T(1,128)S(1)} %get-tuple-element.25.row_ref, bf16[16,4,16,256]{3,2,1,0:T(8,128)(2,1)S(1)} %all_to_all.10.source_ref, bf16[256,256]{1,0:T(8,128)(2,1)S(1)} %copy-done.1, bf16[256,256]{1,0:T(8,128)(2,1)S(1)} %copy-done.2, bf16[256,256]{1,0:T(8,128)(2,1)S(1)} %copy-done.3, ...), custom_call_target="tpu_custom_call" | custom-call | flops 1073741824 | bytes 2097152 | tf_op jit(solution)/shard_map/cross/pallas_call | solution.py:415
  55.9 14.9 %all_to_all.11.returned_ref = bf16[16,4,16,256]{3,2,1,0:T(8,128)(2,1)S(1)} all-to-all(bf16[16,4,16,256]{3,2,1,0:T(8,128)(2,1)S(1)} %cross.1), channel_id=1, replica_groups=mesh['stream'=16,'azim'=4,'slab'=4] {'azim','slab'}, dimensions={0} | all-to-all | bytes 1048576 | tf_op jit(solution)/shard_map/all_to_all | solution.py:426
  70.8 1.1 %final.1 = bf16[4,256,256]{2,1,0:T(8,128)(2,1)} custom-call(bf16[16,4,16,256]{3,2,1,0:T(8,128)(2,1)S(1)} %all_to_all.11.returned_ref, bf16[2,256,256]{2,1,0:T(8,128)(2,1)S(1)} %get-tuple-element.43.refs_0_, bf16[2,256,256]{2,1,0:T(8,128)(2,1)S(1)} %get-tuple-element.44.refs_1_, bf16[256,256]{1,0:T(8,128)(2,1)S(1)} %copy-done), custom_call_target="tpu_custom_call" | custom-call | flops 134217728 | bytes 1572864 | tf_op jit(solution)/shard_map/final/pallas_call | solution.py:428
  (12 shorter events, 0.0 us)
Async XLA Ops:
  1.0 14.1 %collective-permute-start.4 = (bf16[2,256,256]{2,1,0:T(8,128)(2,1)S(1)}, bf16[2,256,256]{2,1,0:T(8,128)(2,1)S(1)}, u32[]{:S(2)}, u32[]{:S(2)}) collective-permute-start(bf16[2,256,256]{2,1,0:T(8,128)(2,1)S(1)} %slice_bitcast_fusion), channel_id=1, source_target_pairs={{240,0},{0,16},{16,32},{32,48},{48,64},{64,80},{80,96},{96,112},{1... | collective-permute-start | bytes 786440 | tf_op jit(solution)/shard_map/ppermute | solution.py:34
  3.5 11.6 %collective-permute-start.5 = (bf16[2,256,256]{2,1,0:T(8,128)(2,1)S(1)}, bf16[2,256,256]{2,1,0:T(8,128)(2,1)S(1)}, u32[]{:S(2)}, u32[]{:S(2)}) collective-permute-start(bf16[2,256,256]{2,1,0:T(8,128)(2,1)S(1)} %slice_bitcast_fusion), channel_id=1, source_target_pairs={{16,0},{32,16},{48,32},{64,48},{80,64},{96,80},{112,96},{128,112},... | collective-permute-start | bytes 786440 | tf_op jit(solution)/shard_map/ppermute | solution.py:34
  9.5 10.6 %collective-permute-start = (bf16[2,256,256]{2,1,0:T(8,128)(2,1)S(1)}, bf16[2,256,256]{2,1,0:T(8,128)(2,1)S(1)}, u32[]{:S(2)}, u32[]{:S(2)}) collective-permute-start(bf16[2,256,256]{2,1,0:T(8,128)(2,1)S(1)} %slice.11), channel_id=1, source_target_pairs={{240,0},{0,16},{16,32},{32,48},{48,64},{64,80},{80,96},{96,112},{1... | collective-permute-start | bytes 786440 | tf_op jit(solution)/shard_map/ppermute | solution.py:34
  9.6 10.5 %collective-permute-start.1 = (bf16[2,256,256]{2,1,0:T(8,128)(2,1)S(1)}, bf16[2,256,256]{2,1,0:T(8,128)(2,1)S(1)}, u32[]{:S(2)}, u32[]{:S(2)}) collective-permute-start(bf16[2,256,256]{2,1,0:T(8,128)(2,1)S(1)} %slice.11), channel_id=1, source_target_pairs={{16,0},{32,16},{48,32},{64,48},{80,64},{96,80},{112,96},{128,112},... | collective-permute-start | bytes 786440 | tf_op jit(solution)/shard_map/ppermute | solution.py:34
  15.1 10.9 %collective-permute-start.6 = (bf16[2,256,256]{2,1,0:T(8,128)(2,1)S(1)}, bf16[2,256,256]{2,1,0:T(8,128)(2,1)S(1)}, u32[]{:S(2)}, u32[]{:S(2)}) collective-permute-start(bf16[2,256,256]{2,1,0:T(8,128)(2,1)S(1)} %collective-permute-done.4.prev_ref), channel_id=1, source_target_pairs={{240,0},{0,16},{16,32},{32,48},{48,64},{64,80},{80,96},{96,112},{1... | collective-permute-start | bytes 786440 | tf_op jit(solution)/shard_map/ppermute | solution.py:34
  15.2 10.8 %collective-permute-start.7 = (bf16[2,256,256]{2,1,0:T(8,128)(2,1)S(1)}, bf16[2,256,256]{2,1,0:T(8,128)(2,1)S(1)}, u32[]{:S(2)}, u32[]{:S(2)}) collective-permute-start(bf16[2,256,256]{2,1,0:T(8,128)(2,1)S(1)} %collective-permute-done.5.next_ref), channel_id=1, source_target_pairs={{16,0},{32,16},{48,32},{64,48},{80,64},{96,80},{112,96},{128,112},... | collective-permute-start | bytes 786440 | tf_op jit(solution)/shard_map/ppermute | solution.py:34
  20.1 11.0 %collective-permute-start.2 = (bf16[2,256,256]{2,1,0:T(8,128)(2,1)S(1)}, bf16[2,256,256]{2,1,0:T(8,128)(2,1)S(1)}, u32[]{:S(2)}, u32[]{:S(2)}) collective-permute-start(bf16[2,256,256]{2,1,0:T(8,128)(2,1)S(1)} %collective-permute-done.prev_ref), channel_id=1, source_target_pairs={{240,0},{0,16},{16,32},{32,48},{48,64},{64,80},{80,96},{96,112},{1... | collective-permute-start | bytes 786440 | tf_op jit(solution)/shard_map/ppermute | solution.py:34
  20.1 11.0 %collective-permute-start.3 = (bf16[2,256,256]{2,1,0:T(8,128)(2,1)S(1)}, bf16[2,256,256]{2,1,0:T(8,128)(2,1)S(1)}, u32[]{:S(2)}, u32[]{:S(2)}) collective-permute-start(bf16[2,256,256]{2,1,0:T(8,128)(2,1)S(1)} %collective-permute-done.1.next_ref), channel_id=1, source_target_pairs={{16,0},{32,16},{48,32},{64,48},{80,64},{96,80},{112,96},{128,112},... | collective-permute-start | bytes 786440 | tf_op jit(solution)/shard_map/ppermute | solution.py:34
  31.1 22.0 %copy-start.1 = (bf16[256,256]{1,0:T(8,128)(2,1)S(1)}, bf16[256,256]{1,0:T(8,128)(2,1)}, u32[]{:S(2)}) copy-start(bf16[256,256]{1,0:T(8,128)(2,1)} %query_weight_ref.1) | copy-start | bytes 393220
  31.1 22.0 %copy-start.2 = (bf16[256,256]{1,0:T(8,128)(2,1)S(1)}, bf16[256,256]{1,0:T(8,128)(2,1)}, u32[]{:S(2)}) copy-start(bf16[256,256]{1,0:T(8,128)(2,1)} %key_weight_ref.1) | copy-start | bytes 393220
  31.1 22.0 %copy-start.3 = (bf16[256,256]{1,0:T(8,128)(2,1)S(1)}, bf16[256,256]{1,0:T(8,128)(2,1)}, u32[]{:S(2)}) copy-start(bf16[256,256]{1,0:T(8,128)(2,1)} %value_weight_ref.1) | copy-start | bytes 393220
  53.2 17.7 %copy-start = (bf16[256,256]{1,0:T(8,128)(2,1)S(1)}, bf16[256,256]{1,0:T(8,128)(2,1)}, u32[]{:S(2)}) copy-start(bf16[256,256]{1,0:T(8,128)(2,1)} %refs_2_.3) | copy-start | bytes 393220

commit v3 on v2

--- a/solution.py
+++ b/solution.py
@@ -23,8 +23,6 @@
 STREAM_MIB = 24
 CROSS_MIB = 24
 FINAL_MIB = 16
-LANES = 128
-SIDES = D // LANES
 F32 = jnp.float32
 BF16 = jnp.bfloat16
 
@@ -65,11 +63,8 @@
     return jnp.concatenate([jnp.where(lane == h, queries, zero) for h in range(HEADS)], axis=0)
 
 
-def attend(stack, keys, values, bias):
-    scores = dot_t(stack, keys)
-    if bias is not None:
-        scores = scores + bias
-    weights = jnp.exp2(scores)
+def attend(stack, keys, values):
+    weights = jnp.exp2(dot_t(stack, keys))
     factors = 1.0 / jnp.sum(weights, axis=-1, keepdims=True)
     summed = dot(weights.astype(BF16), values)
     count = stack.shape[0] // HEADS
@@ -111,12 +106,12 @@
             named = list_ref[block, j]
             section = lax.rem(named // BLOCKS_DEV + (REACH + size) - position_ref[0], size)
             start_ref[block, j] = section * (BLOCKS_DEV * BLOCK) + (named % BLOCKS_DEV) * BLOCK
-    shape = (2 * HEAD_DIM, 2 * HEAD_DIM)
+    tokens = bias_ref.shape[0]
     azimuths = order_ref.shape[0]
 
     def placed(axis):
-        dims = (shape[0], 1) if axis == 0 else (1, shape[1])
-        row = per_azim(lax.broadcasted_iota(jnp.int32, dims, axis) % HEAD_DIM)
+        dims = (tokens, 1) if axis == 0 else (1, HEADS * tokens)
+        row = per_azim(lax.broadcasted_iota(jnp.int32, dims, axis) % tokens)
         found = jnp.zeros(dims, jnp.int32)
         for a in range(azimuths):
             found = jnp.where(row == a, order_ref[a], found)
@@ -124,15 +119,14 @@
 
     distance = placed(0) - placed(1)
     distance = jnp.where(distance < 0, distance + azimuths, distance)
-    same = (lax.broadcasted_iota(jnp.int32, shape, 0) // HEAD_DIM) == (
-        lax.broadcasted_iota(jnp.int32, shape, 1) // HEAD_DIM
-    )
-    distance = jnp.where(same, distance, -1)
-    for h in range(HEADS):
-        value = jnp.full(shape, -1e30, F32)
-        for m in range(azimuths):
-            value = jnp.where(distance == m, table_ref[h, m] * LOG2E, value)
-        bias_ref[h * shape[0] : (h + 1) * shape[0]] = value
+    head = lax.broadcasted_iota(jnp.int32, (1, HEADS * tokens), 1) // tokens
+    value = jnp.zeros(bias_ref.shape, F32)
+    for m in range(azimuths):
+        row = jnp.zeros((1, HEADS * tokens), F32)
+        for h in range(HEADS):
+            row = jnp.where(head == h, table_ref[h, m] * LOG2E, row)
+        value = jnp.where(distance == m, row, value)
+    bias_ref[...] = value
     for copy in copies[5:]:
         copy.wait()
 
@@ -161,6 +155,10 @@
         out_ref[:, at, :D] = keys[part * half : (part + 1) * half].reshape(lines, length, D)
         out_ref[:, at, D:] = values[part * half : (part + 1) * half].reshape(lines, length, D)
     out_ref[:, length : 2 * length] = own_ref[first_line : first_line + lines]
+
+
+def lines_of(ref):
+    return ref.shape[0]
 
 
 def stream_kernel(
@@ -178,19 +176,21 @@
     *refs,
     first_line,
 ):
-    after_ref, send_ref, far = refs[-3:]
-    earlier = refs[:-3]
+    after_ref, send_ref, *far = refs[-2 - lines_of(far_prev_ref) :]
+    earlier = refs[: -2 - lines_of(far_prev_ref)]
     lines, length = far_prev_ref.shape[:2]
     groups = head_groups()
-    tokens = jnp.concatenate(
-        [far_prev_ref[...].reshape(-1, D), far_next_ref[...].reshape(-1, D)], axis=0
-    )
-    normed = normed_rows(tokens, gain_ref[...])
-    far[:, :D] = head_units(dot(normed, key_weight_ref[...]), groups).astype(BF16)
-    far[:, D:] = dot(normed, value_weight_ref[...]).astype(BF16)
     near_rows = window_ref.shape[1]
-    parts = []
-    for line in range(lines):
+    group, _, rows, _ = send_ref.shape
+
+    def project(line):
+        tokens = jnp.concatenate([far_prev_ref[line], far_next_ref[line]], axis=0)
+        normed = normed_rows(tokens, gain_ref[...])
+        far[line][:, :D] = head_units(dot(normed, key_weight_ref[...]), groups).astype(BF16)
+        far[line][:, D:] = dot(normed, value_weight_ref[...]).astype(BF16)
+
+    def attended(line):
+        parts = []
         for block in range(BLOCKS_DEV):
             stack = head_stack(query_ref[first_line + line, block * BLOCK : (block + 1) * BLOCK])
             picked = []
@@ -199,26 +199,32 @@
                 before = start < length
                 after = start >= length + near_rows
                 near_at = jnp.where(before | after, 0, start - length)
-                far_at = line * length + jnp.where(
-                    before, start, jnp.where(after, start - (length + near_rows) + lines * length, 0)
-                )
+                far_at = jnp.where(before, start, jnp.where(after, start - near_rows, 0))
                 close = window_ref[line, pl.ds(pl.multiple_of(near_at, BLOCK), BLOCK)]
-                distant = far[pl.ds(pl.multiple_of(far_at, BLOCK), BLOCK)]
+                distant = far[line][pl.ds(pl.multiple_of(far_at, BLOCK), BLOCK)]
                 picked.append(jnp.where(before | after, distant, close))
             listed = jnp.concatenate(picked, axis=0)
-            parts.append(attend(stack, listed[:, :D], listed[:, D:], None))
-    attended = jnp.concatenate(parts, axis=0).astype(BF16)
-    fields = field_ref[first_line : first_line + lines].reshape(-1, D).astype(F32)
-    after = (fields + dot(attended, out_weight_ref[...])).astype(BF16)
-    after_ref[...] = after.reshape(lines, length, D)
-    normed = normed_rows(after, gain_cross_ref[...])
-    group, _, rows, _ = send_ref.shape
+            parts.append(attend(stack, listed[:, :D], listed[:, D:]))
+        return jnp.concatenate(parts, axis=0).astype(BF16)
+
+    def finish(some, rows_in):
+        fields = field_ref[first_line + some.start : first_line + some.stop].reshape(-1, D).astype(F32)
+        after = (fields + dot(rows_in, out_weight_ref[...])).astype(BF16)
+        after_ref[some] = after.reshape(-1, length, D)
+        normed = normed_rows(after, gain_cross_ref[...])
+        for line in range(some.start, some.stop):
+            at = (line - some.start) * length
+            send_ref[:, first_line + line] = normed[at : at + length].reshape(group, rows, D)
+
     for line in range(lines):
-        send_ref[:, first_line + line] = normed[line * length : (line + 1) * length].reshape(
-            group, rows, D
-        )
+        project(line)
+    finish(slice(0, lines), jnp.concatenate([attended(line) for line in range(lines)], axis=0))
     for previous in earlier:
         send_ref[:, :first_line] = previous[:, :first_line]
+
+
+def turned(block, turn, rows):
+    return dot(turn, block.reshape(rows * rows, D)).astype(BF16)
 
 
 def cross_kernel(
@@ -229,41 +235,43 @@
     value_weight_ref,
     bias_ref,
     out_ref,
-    mixed,
     ordered,
-    query_buffer,
-    key_buffer,
-    value_buffer,
 ):
     groups = head_groups()
     group, line_count, rows = out_ref.shape[:3]
     tokens = group * line_count
-    block = source_ref[...].reshape(tokens * rows, D).astype(F32)
-    for side in range(SIDES):
-        mixed[side] = block[:, side * LANES : (side + 1) * LANES]
-    for index in range(rows):
-        at = slice(index * tokens, (index + 1) * tokens)
-        ordered[at] = jnp.concatenate(
-            [mixed[side, pl.ds(index, tokens, stride=rows)] for side in range(SIDES)], axis=1
-        ).astype(BF16)
-    normed = ordered[...]
-    key_buffer[...] = head_units(dot(normed, key_weight_ref[...]), groups).astype(BF16)
-    query_buffer[...] = (
-        head_units(dot(normed, query_weight_ref[...]), groups) * row_ref[...]
+    square = rows * rows
+    to_row = lax.broadcasted_iota(jnp.int32, (square, square), 0)
+    from_row = lax.broadcasted_iota(jnp.int32, (square, square), 1)
+    turn = jnp.where(from_row == (to_row % rows) * rows + to_row // rows, 1.0, 0.0).astype(BF16)
+    source = source_ref[...].reshape(tokens * rows, D)
+    joint = lax.broadcasted_iota(jnp.int32, (HEADS * tokens, D), 0) // tokens
+    summing = jnp.where(
+        joint == lax.broadcasted_iota(jnp.int32, (HEADS * tokens, D), 1) // HEAD_DIM, 1.0, 0.0
     ).astype(BF16)
-    value_buffer[...] = dot(normed, value_weight_ref[...]).astype(BF16)
-    for pair in range(rows // 2):
-        at = slice(2 * pair * tokens, (2 * pair + 2) * tokens)
-        attended = attend(
-            head_stack(query_buffer[at]), key_buffer[at], value_buffer[at], bias_ref[...]
+    for at in range(0, tokens, rows):
+        block = turned(source[at * rows : (at + rows) * rows], turn, rows)
+        ordered[:, at : at + rows] = block.reshape(rows, rows, D)
+    normed = ordered[...].reshape(rows * tokens, D)
+    keys = head_units(dot(normed, key_weight_ref[...]), groups).astype(BF16)
+    queries = (head_units(dot(normed, query_weight_ref[...]), groups) * row_ref[...]).astype(BF16)
+    values = dot(normed, value_weight_ref[...]).astype(BF16)
+    spans = [slice(index * tokens, (index + 1) * tokens) for index in range(rows)]
+    weights = []
+    for at in spans:
+        scores = dot_t(queries[at], head_stack(keys[at])) + bias_ref[...]
+        weights.append(jnp.exp2(scores).astype(BF16))
+    totals = dot(jnp.concatenate(weights, axis=0), summing)
+    summed = jnp.concatenate(
+        [dot(part, head_stack(values[at])) for part, at in zip(weights, spans)], axis=0
+    )
+    ordered[...] = (summed / totals).astype(BF16).reshape(rows, tokens, D)
+    lines = rows // line_count
+    for at in range(0, tokens, rows):
+        block = turned(ordered[:, at : at + rows], turn, rows)
+        out_ref[at // line_count : at // line_count + lines] = block.reshape(
+            lines, line_count, rows, D
         )
-        for i in range(2):
-            for side in range(SIDES):
-                mixed[side, pl.ds(2 * pair + i, tokens, stride=rows)] = attended[
-                    i * tokens : (i + 1) * tokens, side * LANES : (side + 1) * LANES
-                ]
-    joined = jnp.concatenate([mixed[side] for side in range(SIDES)], axis=1)
-    out_ref[...] = joined.astype(BF16).reshape(out_ref.shape)
 
 
 def final_kernel(returned_ref, *refs):
@@ -331,7 +339,7 @@
 
     def per_azim(token):
         device = token // line_count
-        return (device // slabs) * field.shape[0] + (token % line_count) // lines_per
+        return (device % azims) * field.shape[0] + (token % line_count) // lines_per
 
     shape = jax.ShapeDtypeStruct
     small = [stream_scale, cross_scale, azim_order, azim_bias, block_lists]
@@ -344,7 +352,7 @@
             shape((1, D), F32),
             shape((1, D), F32),
             shape(block_lists.shape, jnp.int32),
-            shape((HEADS * 2 * HEAD_DIM, 2 * HEAD_DIM), F32),
+            shape((group * line_count, HEADS * group * line_count), F32),
         ]
         + [shape(array.shape, array.dtype) for array in fetched],
         scratch_shapes=[pltpu.SMEM(array.shape, array.dtype) for array in small]
@@ -391,7 +399,7 @@
             in_specs=[SMEM] + [VMEM] * (10 + len(send)),
             out_specs=[VMEM] * 2,
             out_shape=[shape((lines, length, D), BF16), shape((group, line_count, rows, D), BF16)],
-            scratch_shapes=[pltpu.VMEM((2 * lines * length, 2 * D), BF16)],
+            scratch_shapes=[pltpu.VMEM((2 * length, 2 * D), BF16)] * lines,
             compiler_params=params(STREAM_MIB),
             cost_estimate=cost(3 << 29, 1 << 22, 1 << 20),
             name="stream",
@@ -411,19 +419,18 @@
         )
         afters.append(after)
 
-    arrived = lax.all_to_all(send[0], ("azim", "slab"), 0, 0, tiled=True)
+    arrived = lax.all_to_all(send[0], ("slab", "azim"), 0, 0, tiled=True)
     crossed = pl.pallas_call(
         cross_kernel,
         in_specs=[VMEM] * 6,
         out_specs=VMEM,
         out_shape=shape((group, line_count, rows, D), BF16),
-        scratch_shapes=[pltpu.VMEM((SIDES, group * line_count * rows, LANES), F32)]
-        + [pltpu.VMEM((group * line_count * rows, D), BF16)] * 4,
+        scratch_shapes=[pltpu.VMEM((rows, group * line_count, D), BF16)],
         compiler_params=params(CROSS_MIB),
         cost_estimate=cost(1 << 30, 1 << 21, 1 << 19),
         name="cross",
     )(cross_row, arrived, cross_query, cross_key, cross_value, bias)
-    returned = lax.all_to_all(crossed, ("azim", "slab"), 0, 0, tiled=True)
+    returned = lax.all_to_all(crossed, ("slab", "azim"), 0, 0, tiled=True)
 
     result = pl.pallas_call(
         final_kernel,

time: 72.2 us -> 71.3 us (0.988)
  no operation moved by 1% of the time
where the time goes in v3:
time: 71.3 us; the launch traced here: 71.1 us
  blocking collectives  33.6 us (47%)
  starting transfers between devices  18.4 us (26%)
  Pallas kernels  13.3 us (19%)
  waiting for transfers between devices  3.61 us (5%)
  local copies, waits for them, and re-layouts  1.95 us (3%)
    all_to_all x1, blocking collectives, per_device(): arrived = lax.all_to_all(send[0], ('slab', 'azim'), 0, 0, tiled=True)  18.6 us
    ppermute x8, starting transfers between devices, shifted(): lax.ppermute(block, 'stream', [((i - distance) % size, i) for i in range(...  18.4 us
    all_to_all x1, blocking collectives, per_device(): returned = lax.all_to_all(crossed, ('slab', 'azim'), 0, 0, tiled=True)  15 us
    pallas_call x2, Pallas kernels, per_device(): pl.pallas_call(functools.partial(stream_kernel, first_line=c * lines), in...  5.63 us
    ppermute x8, waiting for transfers between devices, shifted(): lax.ppermute(block, 'stream', [((i - distance) % size, i) for i in range(...  3.61 us
    pallas_call x1, Pallas kernels, per_device(): pl.pallas_call(cross_kernel, in_specs=[VMEM] * 6, out_specs=VMEM, out_sha...  2.38 us
    pallas_call x1, Pallas kernels, per_device(): pl.pallas_call(functools.partial(prepare_kernel, per_azim=per_azim, size=...  1.92 us
  transfers between devices with their start and end apart: 8, of which 2 were waited for; matrix products, arithmetic and copies ran while one was open for 1% of the time, Pallas kernels for 10%

profile of v3, /device:TPU:1, one launch (start us, length us, event | category | flops | bytes accessed | tf_op | source)
XLA Modules:
  0.0 71.1 jit_solution(12378268571660813643)
XLA Ops:
  0.0 1.0 %slice_bitcast_fusion = bf16[2,256,256]{2,1,0:T(8,128)(2,1)S(1)} fusion(bf16[2,2,256,256]{3,2,1,0:T(8,128)(2,1)} %param.16), kind=kLoop, calls=%fused_computation | loop fusion | bytes 524288 | tf_op jit(solution)/shard_map/slice | solution.py:329
  1.0 2.5 %collective-permute-start.4 = (bf16[2,256,256]{2,1,0:T(8,128)(2,1)S(1)}, bf16[2,256,256]{2,1,0:T(8,128)(2,1)S(1)}, u32[]{:S(2)}, u32[]{:S(2)}) collective-permute-start(bf16[2,256,256]{2,1,0:T(8,128)(2,1)S(1)} %slice_bitcast_fusion), channel_id=1, source_target_pairs={{240,0},{0,16},{16,32},{32,48},{48,64},{64,80},{80,96},{96,112},{1... | collective-permute-start | bytes 786440 | tf_op jit(solution)/shard_map/ppermute | solution.py:32
  3.5 5.0 %collective-permute-start.5 = (bf16[2,256,256]{2,1,0:T(8,128)(2,1)S(1)}, bf16[2,256,256]{2,1,0:T(8,128)(2,1)S(1)}, u32[]{:S(2)}, u32[]{:S(2)}) collective-permute-start(bf16[2,256,256]{2,1,0:T(8,128)(2,1)S(1)} %slice_bitcast_fusion), channel_id=1, source_target_pairs={{16,0},{32,16},{48,32},{64,48},{80,64},{96,80},{112,96},{128,112},... | collective-permute-start | bytes 786440 | tf_op jit(solution)/shard_map/ppermute | solution.py:32
  8.5 1.0 %slice.11 = bf16[2,256,256]{2,1,0:T(8,128)(2,1)S(1)} slice(bf16[4,256,256]{2,1,0:T(8,128)(2,1)} %bitcast.7), slice={[2:4], [0:256], [0:256]} | slice | bytes 524288 | tf_op jit(solution)/shard_map/slice | solution.py:332
  9.5 0.1 collective-permute-start
  9.6 3.6 %collective-permute-start.1 = (bf16[2,256,256]{2,1,0:T(8,128)(2,1)S(1)}, bf16[2,256,256]{2,1,0:T(8,128)(2,1)S(1)}, u32[]{:S(2)}, u32[]{:S(2)}) collective-permute-start(bf16[2,256,256]{2,1,0:T(8,128)(2,1)S(1)} %slice.11), channel_id=1, source_target_pairs={{16,0},{32,16},{48,32},{64,48},{80,64},{96,80},{112,96},{128,112},... | collective-permute-start | bytes 786440 | tf_op jit(solution)/shard_map/ppermute | solution.py:32
  13.2 1.9 %prepare.1 = (f32[1,256]{1,0:T(1,128)S(1)}, f32[1,256]{1,0:T(1,128)S(1)}, s32[2,4]{1,0:T(2,128)S(1)}, f32[64,256]{1,0:T(8,128)S(1)}, bf16[4,256,256]{2,1,0:T(8,1...) custom-call(s32[1]{0:T(128)} %bitcast.position_ref, ...), custom_call_target="tpu_custom_call" | custom-call | flops 1048576 | bytes 262144 | tf_op jit(solution)/shard_map/prepare/pallas_call | solution.py:347
  15.1 0.0 collective-permute-done.4.prev_ref
  15.1 0.1 collective-permute-start.6
  15.2 3.6 %collective-permute-start.7 = (bf16[2,256,256]{2,1,0:T(8,128)(2,1)S(1)}, bf16[2,256,256]{2,1,0:T(8,128)(2,1)S(1)}, u32[]{:S(2)}, u32[]{:S(2)}) collective-permute-start(bf16[2,256,256]{2,1,0:T(8,128)(2,1)S(1)} %collective-permute-done.5.next_ref), channel_id=1, source_target_pairs={{16,0},{32,16},{48,32},{64,48},{80,64},{96,80},{112,96},{128,112},... | collective-permute-start | bytes 786440 | tf_op jit(solution)/shard_map/ppermute | solution.py:32
  18.8 1.3 %collective-permute-done.prev_ref = bf16[2,256,256]{2,1,0:T(8,128)(2,1)S(1)} collective-permute-done((bf16[2,256,256]{2,1,0:T(8,128)(2,1)S(1)}, bf16[2,256,256]{2,1,0:T(8,128)(2,1)S(1)}, u32[]{:S(2)}, u32[]{:S(2)}) %collective-permute-start) | collective-permute-done | bytes 262176 | tf_op jit(solution)/shard_map/ppermute | solution.py:32
  20.1 3.6 %collective-permute-start.3 = (bf16[2,256,256]{2,1,0:T(8,128)(2,1)S(1)}, bf16[2,256,256]{2,1,0:T(8,128)(2,1)S(1)}, u32[]{:S(2)}, u32[]{:S(2)}) collective-permute-start(bf16[2,256,256]{2,1,0:T(8,128)(2,1)S(1)} %collective-permute-done.1.next_ref), channel_id=1, source_target_pairs={{16,0},{32,16},{48,32},{64,48},{80,64},{96,80},{112,96},{128,112},... | collective-permute-start | bytes 786440 | tf_op jit(solution)/shard_map/ppermute | solution.py:32
  23.7 1.0 %own.1 = (bf16[4,256,256]{2,1,0:T(8,128)(2,1)S(1)}, bf16[4,256,512]{2,1,0:T(8,128)(2,1)S(1)}) custom-call(f32[1,256]{1,0:T(1,128)S(1)} %get-tuple-element.27.row_ref, bf16[4,256,256]{2,1,0:T(8,128)(2,1)S(1)} %get-tuple-element.28.field_ref, f32[1,256]{1,0:T(1,128)S(1)} %get-tuple-element.29.gain_ref, ...), custom_call_target="tpu_custom_call" | custom-call | flops 536870912 | bytes 2097152 | tf_op jit(solution)/shard_map/own/pallas_call | solution.py:372
  24.6 0.7 near.3.window_ref
  25.3 0.7 near.2.window_ref
  26.0 2.8 %stream.2 = (bf16[2,256,256]{2,1,0:T(8,128)(2,1)S(1)}, bf16[16,4,16,256]{3,2,1,0:T(8,128)(2,1)S(1)}) custom-call(s32[2,4]{1,0:T(2,128)S(1)} %get-tuple-element.26.start_ref, bf16[4,256,256]{2,1,0:T(8,128)(2,1)S(1)} %get-tuple-element.33.query_ref, bf16[4,256,256]{2,1,0:T(8,128)(2,1)S(1)} %get-tuple-element.28.field_ref, ...), custom_call_target="tpu_custom_call" | custom-call | flops 1610612736 | bytes 4194304 | tf_op jit(solution)/shard_map/stream/pallas_call | solution.py:397
  28.8 2.3 %collective-permute-done.2.far_prev_ref = bf16[2,256,256]{2,1,0:T(8,128)(2,1)S(1)} collective-permute-done((bf16[2,256,256]{2,1,0:T(8,128)(2,1)S(1)}, bf16[2,256,256]{2,1,0:T(8,128)(2,1)S(1)}, u32[]{:S(2)}, u32[]{:S(2)}) %collective-permute-start.2) | collective-permute-done | bytes 262176 | tf_op jit(solution)/shard_map/ppermute | solution.py:32
  31.1 0.0 collective-permute-done.3.far_next_ref
  31.1 2.8 %stream.3 = (bf16[2,256,256]{2,1,0:T(8,128)(2,1)S(1)}, bf16[16,4,16,256]{3,2,1,0:T(8,128)(2,1)S(1)}) custom-call(s32[2,4]{1,0:T(2,128)S(1)} %get-tuple-element.26.start_ref, bf16[4,256,256]{2,1,0:T(8,128)(2,1)S(1)} %get-tuple-element.33.query_ref, bf16[4,256,256]{2,1,0:T(8,128)(2,1)S(1)} %get-tuple-element.28.field_ref, ...), custom_call_target="tpu_custom_call" | custom-call | flops 1610612736 | bytes 4194304 | tf_op jit(solution)/shard_map/stream/pallas_call | solution.py:397
  34.0 18.6 %all_to_all.10.source_ref = bf16[16,4,16,256]{3,2,1,0:T(8,128)(2,1)S(1)} all-to-all(bf16[16,4,16,256]{3,2,1,0:T(8,128)(2,1)S(1)} %get-tuple-element.41), channel_id=1, replica_groups=mesh['stream'=16,'azim'=4,'slab'=4] {'slab','azim'}, dimensions={0} | all-to-all | bytes 1048576 | tf_op jit(solution)/shard_map/all_to_all | solution.py:422
  52.5 0.0 copy-start
  52.6 2.4 %cross.1 = bf16[16,4,16,256]{3,2,1,0:T(8,128)(2,1)S(1)} custom-call(f32[1,256]{1,0:T(1,128)S(1)} %get-tuple-element.25.row_ref, bf16[16,4,16,256]{3,2,1,0:T(8,128)(2,1)S(1)} %all_to_all.10.source_ref, bf16[256,256]{1,0:T(8,128)(2,1)S(1)} %copy-done.1, bf16[256,256]{1,0:T(8,128)(2,1)S(1)} %copy-done.2, bf16[256,256]{1,0:T(8,128)(2,1)S(1)} %copy-done.3, ...), custom_call_target="tpu_custom_call" | custom-call | flops 1073741824 | bytes 2097152 | tf_op jit(solution)/shard_map/cross/pallas_call | solution.py:423
  54.9 15.0 %all_to_all.11.returned_ref = bf16[16,4,16,256]{3,2,1,0:T(8,128)(2,1)S(1)} all-to-all(bf16[16,4,16,256]{3,2,1,0:T(8,128)(2,1)S(1)} %cross.1), channel_id=1, replica_groups=mesh['stream'=16,'azim'=4,'slab'=4] {'slab','azim'}, dimensions={0} | all-to-all | bytes 1048576 | tf_op jit(solution)/shard_map/all_to_all | solution.py:433
  70.0 1.1 %final.1 = bf16[4,256,256]{2,1,0:T(8,128)(2,1)} custom-call(bf16[16,4,16,256]{3,2,1,0:T(8,128)(2,1)S(1)} %all_to_all.11.returned_ref, bf16[2,256,256]{2,1,0:T(8,128)(2,1)S(1)} %get-tuple-element.43.refs_0_, bf16[2,256,256]{2,1,0:T(8,128)(2,1)S(1)} %get-tuple-element.44.refs_1_, bf16[256,256]{1,0:T(8,128)(2,1)S(1)} %copy-done), custom_call_target="tpu_custom_call" | custom-call | flops 134217728 | bytes 1572864 | tf_op jit(solution)/shard_map/final/pallas_call | solution.py:435
  (12 shorter events, 0.0 us)
Async XLA Ops:
  1.0 14.1 %collective-permute-start.4 = (bf16[2,256,256]{2,1,0:T(8,128)(2,1)S(1)}, bf16[2,256,256]{2,1,0:T(8,128)(2,1)S(1)}, u32[]{:S(2)}, u32[]{:S(2)}) collective-permute-start(bf16[2,256,256]{2,1,0:T(8,128)(2,1)S(1)} %slice_bitcast_fusion), channel_id=1, source_target_pairs={{240,0},{0,16},{16,32},{32,48},{48,64},{64,80},{80,96},{96,112},{1... | collective-permute-start | bytes 786440 | tf_op jit(solution)/shard_map/ppermute | solution.py:32
  3.5 11.6 %collective-permute-start.5 = (bf16[2,256,256]{2,1,0:T(8,128)(2,1)S(1)}, bf16[2,256,256]{2,1,0:T(8,128)(2,1)S(1)}, u32[]{:S(2)}, u32[]{:S(2)}) collective-permute-start(bf16[2,256,256]{2,1,0:T(8,128)(2,1)S(1)} %slice_bitcast_fusion), channel_id=1, source_target_pairs={{16,0},{32,16},{48,32},{64,48},{80,64},{96,80},{112,96},{128,112},... | collective-permute-start | bytes 786440 | tf_op jit(solution)/shard_map/ppermute | solution.py:32
  9.5 10.6 %collective-permute-start = (bf16[2,256,256]{2,1,0:T(8,128)(2,1)S(1)}, bf16[2,256,256]{2,1,0:T(8,128)(2,1)S(1)}, u32[]{:S(2)}, u32[]{:S(2)}) collective-permute-start(bf16[2,256,256]{2,1,0:T(8,128)(2,1)S(1)} %slice.11), channel_id=1, source_target_pairs={{240,0},{0,16},{16,32},{32,48},{48,64},{64,80},{80,96},{96,112},{1... | collective-permute-start | bytes 786440 | tf_op jit(solution)/shard_map/ppermute | solution.py:32
  9.6 10.5 %collective-permute-start.1 = (bf16[2,256,256]{2,1,0:T(8,128)(2,1)S(1)}, bf16[2,256,256]{2,1,0:T(8,128)(2,1)S(1)}, u32[]{:S(2)}, u32[]{:S(2)}) collective-permute-start(bf16[2,256,256]{2,1,0:T(8,128)(2,1)S(1)} %slice.11), channel_id=1, source_target_pairs={{16,0},{32,16},{48,32},{64,48},{80,64},{96,80},{112,96},{128,112},... | collective-permute-start | bytes 786440 | tf_op jit(solution)/shard_map/ppermute | solution.py:32
  15.1 10.9 %collective-permute-start.6 = (bf16[2,256,256]{2,1,0:T(8,128)(2,1)S(1)}, bf16[2,256,256]{2,1,0:T(8,128)(2,1)S(1)}, u32[]{:S(2)}, u32[]{:S(2)}) collective-permute-start(bf16[2,256,256]{2,1,0:T(8,128)(2,1)S(1)} %collective-permute-done.4.prev_ref), channel_id=1, source_target_pairs={{240,0},{0,16},{16,32},{32,48},{48,64},{64,80},{80,96},{96,112},{1... | collective-permute-start | bytes 786440 | tf_op jit(solution)/shard_map/ppermute | solution.py:32
  15.2 10.8 %collective-permute-start.7 = (bf16[2,256,256]{2,1,0:T(8,128)(2,1)S(1)}, bf16[2,256,256]{2,1,0:T(8,128)(2,1)S(1)}, u32[]{:S(2)}, u32[]{:S(2)}) collective-permute-start(bf16[2,256,256]{2,1,0:T(8,128)(2,1)S(1)} %collective-permute-done.5.next_ref), channel_id=1, source_target_pairs={{16,0},{32,16},{48,32},{64,48},{80,64},{96,80},{112,96},{128,112},... | collective-permute-start | bytes 786440 | tf_op jit(solution)/shard_map/ppermute | solution.py:32
  20.1 11.0 %collective-permute-start.2 = (bf16[2,256,256]{2,1,0:T(8,128)(2,1)S(1)}, bf16[2,256,256]{2,1,0:T(8,128)(2,1)S(1)}, u32[]{:S(2)}, u32[]{:S(2)}) collective-permute-start(bf16[2,256,256]{2,1,0:T(8,128)(2,1)S(1)} %collective-permute-done.prev_ref), channel_id=1, source_target_pairs={{240,0},{0,16},{16,32},{32,48},{48,64},{64,80},{80,96},{96,112},{1... | collective-permute-start | bytes 786440 | tf_op jit(solution)/shard_map/ppermute | solution.py:32
  20.1 11.0 %collective-permute-start.3 = (bf16[2,256,256]{2,1,0:T(8,128)(2,1)S(1)}, bf16[2,256,256]{2,1,0:T(8,128)(2,1)S(1)}, u32[]{:S(2)}, u32[]{:S(2)}) collective-permute-start(bf16[2,256,256]{2,1,0:T(8,128)(2,1)S(1)} %collective-permute-done.1.next_ref), channel_id=1, source_target_pairs={{16,0},{32,16},{48,32},{64,48},{80,64},{96,80},{112,96},{128,112},... | collective-permute-start | bytes 786440 | tf_op jit(solution)/shard_map/ppermute | solution.py:32
  31.1 21.4 %copy-start.1 = (bf16[256,256]{1,0:T(8,128)(2,1)S(1)}, bf16[256,256]{1,0:T(8,128)(2,1)}, u32[]{:S(2)}) copy-start(bf16[256,256]{1,0:T(8,128)(2,1)} %query_weight_ref.1) | copy-start | bytes 393220
  31.1 21.4 %copy-start.2 = (bf16[256,256]{1,0:T(8,128)(2,1)S(1)}, bf16[256,256]{1,0:T(8,128)(2,1)}, u32[]{:S(2)}) copy-start(bf16[256,256]{1,0:T(8,128)(2,1)} %key_weight_ref.1) | copy-start | bytes 393220
  31.1 21.4 %copy-start.3 = (bf16[256,256]{1,0:T(8,128)(2,1)S(1)}, bf16[256,256]{1,0:T(8,128)(2,1)}, u32[]{:S(2)}) copy-start(bf16[256,256]{1,0:T(8,128)(2,1)} %value_weight_ref.1) | copy-start | bytes 393220
  52.5 17.4 %copy-start = (bf16[256,256]{1,0:T(8,128)(2,1)S(1)}, bf16[256,256]{1,0:T(8,128)(2,1)}, u32[]{:S(2)}) copy-start(bf16[256,256]{1,0:T(8,128)(2,1)} %refs_2_.3) | copy-start | bytes 393220

commit v4 on v3

--- a/solution.py
+++ b/solution.py
@@ -184,10 +184,13 @@
     group, _, rows, _ = send_ref.shape
 
     def project(line):
-        tokens = jnp.concatenate([far_prev_ref[line], far_next_ref[line]], axis=0)
-        normed = normed_rows(tokens, gain_ref[...])
-        far[line][:, :D] = head_units(dot(normed, key_weight_ref[...]), groups).astype(BF16)
-        far[line][:, D:] = dot(normed, value_weight_ref[...]).astype(BF16)
+        tokens = jnp.concatenate([far_prev_ref[line], far_next_ref[line]], axis=0).astype(F32)
+        gained = (tokens * gain_ref[...]).astype(BF16)
+        mean = jnp.mean(tokens * tokens, axis=-1, keepdims=True)
+        factor = lax.rsqrt(mean + 1e-05)
+        keys = dot(gained, key_weight_ref[...]) * factor
+        far[line][:, :D] = head_units(keys, groups).astype(BF16)
+        far[line][:, D:] = (dot(gained, value_weight_ref[...]) * factor).astype(BF16)
 
     def attended(line):
         parts = []

time: 71.3 us -> 71.3 us (level)
  no operation moved by 1% of the time
where the time goes in v4:
time: 71.3 us; the launch traced here: 71 us
  blocking collectives  33.6 us (47%)
  starting transfers between devices  18.4 us (26%)
  Pallas kernels  13.3 us (19%)
  waiting for transfers between devices  3.64 us (5%)
  local copies, waits for them, and re-layouts  1.95 us (3%)
    all_to_all x1, blocking collectives, per_device(): arrived = lax.all_to_all(send[0], ('slab', 'azim'), 0, 0, tiled=True)  18.6 us
    ppermute x8, starting transfers between devices, shifted(): lax.ppermute(block, 'stream', [((i - distance) % size, i) for i in range(...  18.4 us
    all_to_all x1, blocking collectives, per_device(): returned = lax.all_to_all(crossed, ('slab', 'azim'), 0, 0, tiled=True)  15 us
    pallas_call x2, Pallas kernels, per_device(): pl.pallas_call(functools.partial(stream_kernel, first_line=c * lines), in...  5.56 us
    ppermute x8, waiting for transfers between devices, shifted(): lax.ppermute(block, 'stream', [((i - distance) % size, i) for i in range(...  3.64 us
    pallas_call x1, Pallas kernels, per_device(): pl.pallas_call(cross_kernel, in_specs=[VMEM] * 6, out_specs=VMEM, out_sha...  2.39 us
    pallas_call x1, Pallas kernels, per_device(): pl.pallas_call(functools.partial(prepare_kernel, per_azim=per_azim, size=...  1.92 us
  transfers between devices with their start and end apart: 8, of which 2 were waited for; matrix products, arithmetic and copies ran while one was open for 1% of the time, Pallas kernels for 10%

profile of v4, /device:TPU:1, one launch (start us, length us, event | category | flops | bytes accessed | tf_op | source)
XLA Modules:
  0.0 71.0 jit_solution(3900149665100786592)
XLA Ops:
  0.0 1.0 %slice_bitcast_fusion = bf16[2,256,256]{2,1,0:T(8,128)(2,1)S(1)} fusion(bf16[2,2,256,256]{3,2,1,0:T(8,128)(2,1)} %param.16), kind=kLoop, calls=%fused_computation | loop fusion | bytes 524288 | tf_op jit(solution)/shard_map/slice | solution.py:332
  1.0 2.5 %collective-permute-start.4 = (bf16[2,256,256]{2,1,0:T(8,128)(2,1)S(1)}, bf16[2,256,256]{2,1,0:T(8,128)(2,1)S(1)}, u32[]{:S(2)}, u32[]{:S(2)}) collective-permute-start(bf16[2,256,256]{2,1,0:T(8,128)(2,1)S(1)} %slice_bitcast_fusion), channel_id=1, source_target_pairs={{240,0},{0,16},{16,32},{32,48},{48,64},{64,80},{80,96},{96,112},{1... | collective-permute-start | bytes 786440 | tf_op jit(solution)/shard_map/ppermute | solution.py:32
  3.5 5.0 %collective-permute-start.5 = (bf16[2,256,256]{2,1,0:T(8,128)(2,1)S(1)}, bf16[2,256,256]{2,1,0:T(8,128)(2,1)S(1)}, u32[]{:S(2)}, u32[]{:S(2)}) collective-permute-start(bf16[2,256,256]{2,1,0:T(8,128)(2,1)S(1)} %slice_bitcast_fusion), channel_id=1, source_target_pairs={{16,0},{32,16},{48,32},{64,48},{80,64},{96,80},{112,96},{128,112},... | collective-permute-start | bytes 786440 | tf_op jit(solution)/shard_map/ppermute | solution.py:32
  8.5 1.0 %slice.11 = bf16[2,256,256]{2,1,0:T(8,128)(2,1)S(1)} slice(bf16[4,256,256]{2,1,0:T(8,128)(2,1)} %bitcast.7), slice={[2:4], [0:256], [0:256]} | slice | bytes 524288 | tf_op jit(solution)/shard_map/slice | solution.py:335
  9.5 0.1 collective-permute-start
  9.6 3.6 %collective-permute-start.1 = (bf16[2,256,256]{2,1,0:T(8,128)(2,1)S(1)}, bf16[2,256,256]{2,1,0:T(8,128)(2,1)S(1)}, u32[]{:S(2)}, u32[]{:S(2)}) collective-permute-start(bf16[2,256,256]{2,1,0:T(8,128)(2,1)S(1)} %slice.11), channel_id=1, source_target_pairs={{16,0},{32,16},{48,32},{64,48},{80,64},{96,80},{112,96},{128,112},... | collective-permute-start | bytes 786440 | tf_op jit(solution)/shard_map/ppermute | solution.py:32
  13.2 1.9 %prepare.1 = (f32[1,256]{1,0:T(1,128)S(1)}, f32[1,256]{1,0:T(1,128)S(1)}, s32[2,4]{1,0:T(2,128)S(1)}, f32[64,256]{1,0:T(8,128)S(1)}, bf16[4,256,256]{2,1,0:T(8,1...) custom-call(s32[1]{0:T(128)} %bitcast.position_ref, ...), custom_call_target="tpu_custom_call" | custom-call | flops 1048576 | bytes 262144 | tf_op jit(solution)/shard_map/prepare/pallas_call | solution.py:350
  15.1 0.0 collective-permute-done.4.prev_ref
  15.1 0.0 collective-permute-done.5.next_ref
  15.1 0.1 collective-permute-start.6
  15.2 3.6 %collective-permute-start.7 = (bf16[2,256,256]{2,1,0:T(8,128)(2,1)S(1)}, bf16[2,256,256]{2,1,0:T(8,128)(2,1)S(1)}, u32[]{:S(2)}, u32[]{:S(2)}) collective-permute-start(bf16[2,256,256]{2,1,0:T(8,128)(2,1)S(1)} %collective-permute-done.5.next_ref), channel_id=1, source_target_pairs={{16,0},{32,16},{48,32},{64,48},{80,64},{96,80},{112,96},{128,112},... | collective-permute-start | bytes 786440 | tf_op jit(solution)/shard_map/ppermute | solution.py:32
  18.8 1.3 %collective-permute-done.prev_ref = bf16[2,256,256]{2,1,0:T(8,128)(2,1)S(1)} collective-permute-done((bf16[2,256,256]{2,1,0:T(8,128)(2,1)S(1)}, bf16[2,256,256]{2,1,0:T(8,128)(2,1)S(1)}, u32[]{:S(2)}, u32[]{:S(2)}) %collective-permute-start) | collective-permute-done | bytes 262176 | tf_op jit(solution)/shard_map/ppermute | solution.py:32
  20.1 3.6 %collective-permute-start.3 = (bf16[2,256,256]{2,1,0:T(8,128)(2,1)S(1)}, bf16[2,256,256]{2,1,0:T(8,128)(2,1)S(1)}, u32[]{:S(2)}, u32[]{:S(2)}) collective-permute-start(bf16[2,256,256]{2,1,0:T(8,128)(2,1)S(1)} %collective-permute-done.1.next_ref), channel_id=1, source_target_pairs={{16,0},{32,16},{48,32},{64,48},{80,64},{96,80},{112,96},{128,112},... | collective-permute-start | bytes 786440 | tf_op jit(solution)/shard_map/ppermute | solution.py:32
  23.7 1.0 %own.1 = (bf16[4,256,256]{2,1,0:T(8,128)(2,1)S(1)}, bf16[4,256,512]{2,1,0:T(8,128)(2,1)S(1)}) custom-call(f32[1,256]{1,0:T(1,128)S(1)} %get-tuple-element.27.row_ref, bf16[4,256,256]{2,1,0:T(8,128)(2,1)S(1)} %get-tuple-element.28.field_ref, f32[1,256]{1,0:T(1,128)S(1)} %get-tuple-element.29.gain_ref, ...), custom_call_target="tpu_custom_call" | custom-call | flops 536870912 | bytes 2097152 | tf_op jit(solution)/shard_map/own/pallas_call | solution.py:375
  24.6 0.7 near.3.window_ref
  25.3 0.7 near.2.window_ref
  26.0 2.8 %stream.2 = (bf16[2,256,256]{2,1,0:T(8,128)(2,1)S(1)}, bf16[16,4,16,256]{3,2,1,0:T(8,128)(2,1)S(1)}) custom-call(s32[2,4]{1,0:T(2,128)S(1)} %get-tuple-element.26.start_ref, bf16[4,256,256]{2,1,0:T(8,128)(2,1)S(1)} %get-tuple-element.33.query_ref, bf16[4,256,256]{2,1,0:T(8,128)(2,1)S(1)} %get-tuple-element.28.field_ref, ...), custom_call_target="tpu_custom_call" | custom-call | flops 1610612736 | bytes 4194304 | tf_op jit(solution)/shard_map/stream/pallas_call | solution.py:400
  28.8 2.3 %collective-permute-done.2.far_prev_ref = bf16[2,256,256]{2,1,0:T(8,128)(2,1)S(1)} collective-permute-done((bf16[2,256,256]{2,1,0:T(8,128)(2,1)S(1)}, bf16[2,256,256]{2,1,0:T(8,128)(2,1)S(1)}, u32[]{:S(2)}, u32[]{:S(2)}) %collective-permute-start.2) | collective-permute-done | bytes 262176 | tf_op jit(solution)/shard_map/ppermute | solution.py:32
  31.1 2.8 %stream.3 = (bf16[2,256,256]{2,1,0:T(8,128)(2,1)S(1)}, bf16[16,4,16,256]{3,2,1,0:T(8,128)(2,1)S(1)}) custom-call(s32[2,4]{1,0:T(2,128)S(1)} %get-tuple-element.26.start_ref, bf16[4,256,256]{2,1,0:T(8,128)(2,1)S(1)} %get-tuple-element.33.query_ref, bf16[4,256,256]{2,1,0:T(8,128)(2,1)S(1)} %get-tuple-element.28.field_ref, ...), custom_call_target="tpu_custom_call" | custom-call | flops 1610612736 | bytes 4194304 | tf_op jit(solution)/shard_map/stream/pallas_call | solution.py:400
  33.9 18.6 %all_to_all.10.source_ref = bf16[16,4,16,256]{3,2,1,0:T(8,128)(2,1)S(1)} all-to-all(bf16[16,4,16,256]{3,2,1,0:T(8,128)(2,1)S(1)} %get-tuple-element.41), channel_id=1, replica_groups=mesh['stream'=16,'azim'=4,'slab'=4] {'slab','azim'}, dimensions={0} | all-to-all | bytes 1048576 | tf_op jit(solution)/shard_map/all_to_all | solution.py:425
  52.5 0.0 copy-start
  52.5 2.4 %cross.1 = bf16[16,4,16,256]{3,2,1,0:T(8,128)(2,1)S(1)} custom-call(f32[1,256]{1,0:T(1,128)S(1)} %get-tuple-element.25.row_ref, bf16[16,4,16,256]{3,2,1,0:T(8,128)(2,1)S(1)} %all_to_all.10.source_ref, bf16[256,256]{1,0:T(8,128)(2,1)S(1)} %copy-done.1, bf16[256,256]{1,0:T(8,128)(2,1)S(1)} %copy-done.2, bf16[256,256]{1,0:T(8,128)(2,1)S(1)} %copy-done.3, ...), custom_call_target="tpu_custom_call" | custom-call | flops 1073741824 | bytes 2097152 | tf_op jit(solution)/shard_map/cross/pallas_call | solution.py:426
  54.9 15.0 %all_to_all.11.returned_ref = bf16[16,4,16,256]{3,2,1,0:T(8,128)(2,1)S(1)} all-to-all(bf16[16,4,16,256]{3,2,1,0:T(8,128)(2,1)S(1)} %cross.1), channel_id=1, replica_groups=mesh['stream'=16,'azim'=4,'slab'=4] {'slab','azim'}, dimensions={0} | all-to-all | bytes 1048576 | tf_op jit(solution)/shard_map/all_to_all | solution.py:436
  69.9 1.1 %final.1 = bf16[4,256,256]{2,1,0:T(8,128)(2,1)} custom-call(bf16[16,4,16,256]{3,2,1,0:T(8,128)(2,1)S(1)} %all_to_all.11.returned_ref, bf16[2,256,256]{2,1,0:T(8,128)(2,1)S(1)} %get-tuple-element.43.refs_0_, bf16[2,256,256]{2,1,0:T(8,128)(2,1)S(1)} %get-tuple-element.44.refs_1_, bf16[256,256]{1,0:T(8,128)(2,1)S(1)} %copy-done), custom_call_target="tpu_custom_call" | custom-call | flops 134217728 | bytes 1572864 | tf_op jit(solution)/shard_map/final/pallas_call | solution.py:438
  (12 shorter events, 0.0 us)
Async XLA Ops:
  1.0 14.1 %collective-permute-start.4 = (bf16[2,256,256]{2,1,0:T(8,128)(2,1)S(1)}, bf16[2,256,256]{2,1,0:T(8,128)(2,1)S(1)}, u32[]{:S(2)}, u32[]{:S(2)}) collective-permute-start(bf16[2,256,256]{2,1,0:T(8,128)(2,1)S(1)} %slice_bitcast_fusion), channel_id=1, source_target_pairs={{240,0},{0,16},{16,32},{32,48},{48,64},{64,80},{80,96},{96,112},{1... | collective-permute-start | bytes 786440 | tf_op jit(solution)/shard_map/ppermute | solution.py:32
  3.5 11.6 %collective-permute-start.5 = (bf16[2,256,256]{2,1,0:T(8,128)(2,1)S(1)}, bf16[2,256,256]{2,1,0:T(8,128)(2,1)S(1)}, u32[]{:S(2)}, u32[]{:S(2)}) collective-permute-start(bf16[2,256,256]{2,1,0:T(8,128)(2,1)S(1)} %slice_bitcast_fusion), channel_id=1, source_target_pairs={{16,0},{32,16},{48,32},{64,48},{80,64},{96,80},{112,96},{128,112},... | collective-permute-start | bytes 786440 | tf_op jit(solution)/shard_map/ppermute | solution.py:32
  9.5 10.6 %collective-permute-start = (bf16[2,256,256]{2,1,0:T(8,128)(2,1)S(1)}, bf16[2,256,256]{2,1,0:T(8,128)(2,1)S(1)}, u32[]{:S(2)}, u32[]{:S(2)}) collective-permute-start(bf16[2,256,256]{2,1,0:T(8,128)(2,1)S(1)} %slice.11), channel_id=1, source_target_pairs={{240,0},{0,16},{16,32},{32,48},{48,64},{64,80},{80,96},{96,112},{1... | collective-permute-start | bytes 786440 | tf_op jit(solution)/shard_map/ppermute | solution.py:32
  9.6 10.5 %collective-permute-start.1 = (bf16[2,256,256]{2,1,0:T(8,128)(2,1)S(1)}, bf16[2,256,256]{2,1,0:T(8,128)(2,1)S(1)}, u32[]{:S(2)}, u32[]{:S(2)}) collective-permute-start(bf16[2,256,256]{2,1,0:T(8,128)(2,1)S(1)} %slice.11), channel_id=1, source_target_pairs={{16,0},{32,16},{48,32},{64,48},{80,64},{96,80},{112,96},{128,112},... | collective-permute-start | bytes 786440 | tf_op jit(solution)/shard_map/ppermute | solution.py:32
  15.1 10.9 %collective-permute-start.6 = (bf16[2,256,256]{2,1,0:T(8,128)(2,1)S(1)}, bf16[2,256,256]{2,1,0:T(8,128)(2,1)S(1)}, u32[]{:S(2)}, u32[]{:S(2)}) collective-permute-start(bf16[2,256,256]{2,1,0:T(8,128)(2,1)S(1)} %collective-permute-done.4.prev_ref), channel_id=1, source_target_pairs={{240,0},{0,16},{16,32},{32,48},{48,64},{64,80},{80,96},{96,112},{1... | collective-permute-start | bytes 786440 | tf_op jit(solution)/shard_map/ppermute | solution.py:32
  15.2 10.8 %collective-permute-start.7 = (bf16[2,256,256]{2,1,0:T(8,128)(2,1)S(1)}, bf16[2,256,256]{2,1,0:T(8,128)(2,1)S(1)}, u32[]{:S(2)}, u32[]{:S(2)}) collective-permute-start(bf16[2,256,256]{2,1,0:T(8,128)(2,1)S(1)} %collective-permute-done.5.next_ref), channel_id=1, source_target_pairs={{16,0},{32,16},{48,32},{64,48},{80,64},{96,80},{112,96},{128,112},... | collective-permute-start | bytes 786440 | tf_op jit(solution)/shard_map/ppermute | solution.py:32
  20.1 11.0 %collective-permute-start.2 = (bf16[2,256,256]{2,1,0:T(8,128)(2,1)S(1)}, bf16[2,256,256]{2,1,0:T(8,128)(2,1)S(1)}, u32[]{:S(2)}, u32[]{:S(2)}) collective-permute-start(bf16[2,256,256]{2,1,0:T(8,128)(2,1)S(1)} %collective-permute-done.prev_ref), channel_id=1, source_target_pairs={{240,0},{0,16},{16,32},{32,48},{48,64},{64,80},{80,96},{96,112},{1... | collective-permute-start | bytes 786440 | tf_op jit(solution)/shard_map/ppermute | solution.py:32
  20.1 11.0 %collective-permute-start.3 = (bf16[2,256,256]{2,1,0:T(8,128)(2,1)S(1)}, bf16[2,256,256]{2,1,0:T(8,128)(2,1)S(1)}, u32[]{:S(2)}, u32[]{:S(2)}) collective-permute-start(bf16[2,256,256]{2,1,0:T(8,128)(2,1)S(1)} %collective-permute-done.1.next_ref), channel_id=1, source_target_pairs={{16,0},{32,16},{48,32},{64,48},{80,64},{96,80},{112,96},{128,112},... | collective-permute-start | bytes 786440 | tf_op jit(solution)/shard_map/ppermute | solution.py:32
  31.1 21.4 %copy-start.1 = (bf16[256,256]{1,0:T(8,128)(2,1)S(1)}, bf16[256,256]{1,0:T(8,128)(2,1)}, u32[]{:S(2)}) copy-start(bf16[256,256]{1,0:T(8,128)(2,1)} %query_weight_ref.1) | copy-start | bytes 393220
  31.1 21.4 %copy-start.2 = (bf16[256,256]{1,0:T(8,128)(2,1)S(1)}, bf16[256,256]{1,0:T(8,128)(2,1)}, u32[]{:S(2)}) copy-start(bf16[256,256]{1,0:T(8,128)(2,1)} %key_weight_ref.1) | copy-start | bytes 393220
  31.1 21.4 %copy-start.3 = (bf16[256,256]{1,0:T(8,128)(2,1)S(1)}, bf16[256,256]{1,0:T(8,128)(2,1)}, u32[]{:S(2)}) copy-start(bf16[256,256]{1,0:T(8,128)(2,1)} %value_weight_ref.1) | copy-start | bytes 393220
  52.5 17.4 %copy-start = (bf16[256,256]{1,0:T(8,128)(2,1)S(1)}, bf16[256,256]{1,0:T(8,128)(2,1)}, u32[]{:S(2)}) copy-start(bf16[256,256]{1,0:T(8,128)(2,1)} %refs_2_.3) | copy-start | bytes 393220
